TPU v7x, 256 devices: a whole 4x4x8 slice. The times are simulated.
256 devices in a mesh: rows: 64 (over y, x_hi, z), heads: 4 (over x_lo, core).
Axes of the slice: x: 4 (x_hi: 2, x_lo: 2; x = x_hi * 2 + x_lo), y: 4, z: 8, core: 2. Of those that a mesh axis runs over, the one named last changes fastest.
Arguments:
- tokens: bfloat16 [256, 512, 768], P('rows', None, 'heads'), may hold values from -24 to 24
- qkv_weight: bfloat16 [2, 768, 3, 768], replicated, may hold values from -0.21875 to 0.21875
- out_weight: bfloat16 [2, 768, 768], replicated, may hold values from -0.21875 to 0.21875
- norm_gain: bfloat16 [2, 768], replicated, may hold values from 0.099609375 to 1.8984375
Outputs:
- stream: bfloat16 [256, 512, 768], P('rows', None, 'heads')
All inputs are finite; a program needn't handle non-finite values.
Results may differ from a plain program's by a relative error of at most 0.0096.
Values may be sent and summed in bfloat16 or wider, within the bound.
A program may use at most 64 MiB of HBM per device.

v0:
```python
import jax
import jax.numpy as jnp
from jax import lax
from jax.sharding import Mesh
from jax.sharding import PartitionSpec as P

D = 768
HEADS = 12
HEAD_DIM = 64
LAYERS = 2
BLOCKS = 2
HEADS_AXES = ("heads_0", "heads_1")


epsilon = 1e-06


def in_blocks(shard, dim, peers):
    lengths = shard.shape
    pieces = shard.reshape(*lengths[:dim], peers, lengths[dim] // peers, *lengths[dim + 1 :])
    return jnp.moveaxis(pieces, dim, 0)


def sent_and_summed(shard, axis, dim):
    pieces = in_blocks(shard, dim, lax.axis_size(axis))
    arrived = lax.all_to_all(pieces, axis, split_axis=0, concat_axis=0, tiled=True)
    return arrived.sum(axis=0)


def in_order(pieces, dim):
    pieces = jnp.moveaxis(pieces, 0, dim)
    lengths = pieces.shape
    return pieces.reshape(*lengths[:dim], lengths[dim] * lengths[dim + 1], *lengths[dim + 2 :])


def from_everyone(shard, axis):
    peers = lax.axis_size(axis)
    return lax.all_to_all(
        jnp.broadcast_to(shard[None], (peers, *shard.shape)), axis, 0, 0, tiled=True
    )


def gather_directly(shard, axis, dim):
    return in_order(from_everyone(shard, axis), dim)


def turned_blocks(pieces, axes, sequence):
    lengths = [lax.axis_size(a) for a in axes]
    pieces = pieces.reshape(*lengths, *pieces.shape[1:])
    for k in sequence:
        pieces = lax.all_to_all(pieces, axes[k], split_axis=k, concat_axis=k, tiled=True)
    return pieces.reshape(-1, *pieces.shape[len(axes) :])


def core_and_chips(shard, groups, sequence, split_dim, concat_dim):
    peers = lax.axis_size(groups[0]) * lax.axis_size(groups[1])
    pieces = in_blocks(shard, split_dim, peers)
    return in_order(turned_blocks(pieces, groups, sequence), concat_dim)


def attend(projected, score_scale):
    residues = projected.shape[1]
    queries = projected[:, :, 0]
    key_vecs = projected[:, :, 1]
    values = projected[:, :, 2]
    block_rows = residues // BLOCKS
    pieces_out = []
    for block_index in range(BLOCKS):
        block_queries = queries[:, block_index * block_rows : (block_index + 1) * block_rows]
        partial_value = (
            jnp.einsum(
                "sihc,sjhc->hij", block_queries, key_vecs, preferred_element_type=jnp.float32
            )
            * score_scale
        )
        score_share = sent_and_summed(partial_value, "rows", 1)
        local_weights = jax.nn.softmax(score_share, axis=-1).astype(jnp.bfloat16)
        weights = gather_directly(local_weights, "rows", 1)
        attended = jnp.einsum("hij,sjhc->sihc", weights, values, preferred_element_type=jnp.float32)
        pieces_out.append(attended.astype(jnp.bfloat16))
    return jnp.concatenate(pieces_out, axis=1)


def on_device(tokens, qkv_weight, out_weight, norm_gain):
    seq_dev, residues, slice_width = tokens.shape
    score_scale = 1.0 / (HEAD_DIM * seq_dev * lax.axis_size("rows")) ** 0.5
    stream = core_and_chips(tokens, ("heads_0", "heads_1"), (1, 0), 1, 2)
    quarter = stream.shape[1]
    for layer_index in range(LAYERS):
        qkv_matrix = qkv_weight[layer_index].reshape(D, 3 * D)
        projected = jnp.dot(
            stream.reshape(seq_dev * quarter, D), qkv_matrix, preferred_element_type=jnp.float32
        )
        projected = projected.astype(jnp.bfloat16).reshape(seq_dev, quarter, 3, HEADS, HEAD_DIM)
        head_major = lax.all_to_all(projected, HEADS_AXES, split_axis=3, concat_axis=1, tiled=True)
        attended = attend(head_major, score_scale)
        gathered_heads = lax.all_to_all(
            attended, HEADS_AXES, split_axis=1, concat_axis=2, tiled=True
        )
        update = jnp.dot(
            gathered_heads.reshape(seq_dev * quarter, D),
            out_weight[layer_index],
            preferred_element_type=jnp.float32,
        )
        summed = stream.astype(jnp.float32) + update.reshape(seq_dev, quarter, D)
        mean_sq = jnp.mean(summed * summed, axis=-1, keepdims=True)
        normed = summed * lax.rsqrt(mean_sq + epsilon) * norm_gain[layer_index].astype(jnp.float32)
        stream = normed.astype(jnp.bfloat16)
    return lax.all_to_all(stream, HEADS_AXES, split_axis=2, concat_axis=1, tiled=True)


def solution(mesh):
    finer = Mesh(mesh.devices.reshape(mesh.shape["rows"], 2, 2), ("rows", "heads_0", "heads_1"))
    return jax.shard_map(
        on_device,
        mesh=finer,
        in_specs=(P("rows", None, HEADS_AXES), P(), P(), P()),
        out_specs=P("rows", None, HEADS_AXES),
        check_vma=False,
    )
```

profile of v0, /device:TPU:1, one launch (start us, length us, event | category | flops | bytes accessed | tf_op | source)
XLA Modules:
  0.0 554.8 jit_solution(12274515049256920029)
XLA Ops:
  1.9 7.2 %all_to_all.134 = bf16[2,2,4,128,192]{3,4,2,0,1:T(8,128)(2,1)S(1)} all-to-all(bf16[2,2,4,128,192]{3,4,2,0,1:T(8,128)(2,1)S(1)} %copy.110), channel_id=1, replica_groups=mesh['rows'=64,'heads_0'=2,'heads_1'=2] {'heads_1'}, dimensions={1} | all-to-all | bytes 1572864 | tf_op jit(solution)/shard_map/all_to_all | solution.py:51
  19.7 6.0 %copy.160 = bf16[1,768,3,768]{1,3,2,0:T(8,128)(2,1)} copy(bf16[1,768,3,768]{3,1,2,0:T(8,128)(2,1)} %get-tuple-element.8) | data formatting | bytes 7077888
  27.5 5.5 convolution_convert_fusion.1
  45.7 30.9 %all_to_all.135 = bf16[4,128,3,12,64]{1,0,4,2,3:T(4,128)(2,1)S(1)} all-to-all(bf16[4,128,3,12,64]{1,0,4,2,3:T(4,128)(2,1)S(1)} %copy.116), channel_id=1, replica_groups=mesh['rows'=64,'heads_0'=2,'heads_1'=2] {'heads_0','heads_1'}, dimensions={3} | all-to-all | bytes 4718592 | tf_op jit(solution)/shard_map/all_to_all | solution.py:95
  96.3 12.8 %all-to-all-start.3 = ((f32[64,3,4,512]{3,2,1,0:T(4,128)}), f32[64,3,4,512]{3,2,1,0:T(4,128)}, u32[]{:S(2)}, u32[]{:S(2)}) async-start(f32[64,3,4,512]{3,2,1,0:T(4,128)} %bitcast.148), calls=%async_computation.3 | async-start | bytes 3145728 | tf_op jit(solution)/shard_map/all_to_all | solution.py:26
  117.6 29.6 %all-to-all-done.3 = f32[64,3,4,512]{3,2,1,0:T(4,128)} async-done(((f32[64,3,4,512]{3,2,1,0:T(4,128)}), f32[64,3,4,512]{3,2,1,0:T(4,128)}, u32[]{:S(2)}, u32[]{:S(2)}) %all-to-all-start.3) | async-done | bytes 1572896 | tf_op jit(solution)/shard_map/all_to_all | solution.py:26
  147.2 8.9 %all-to-all-start.5 = ((f32[64,3,4,512]{3,2,1,0:T(4,128)}), f32[64,3,4,512]{3,2,1,0:T(4,128)}, u32[]{:S(2)}, u32[]{:S(2)}) async-start(f32[64,3,4,512]{3,2,1,0:T(4,128)} %bitcast.146), calls=%async_computation.5 | async-start | bytes 3145728 | tf_op jit(solution)/shard_map/all_to_all | solution.py:26
  159.4 34.0 %all-to-all-done.5 = f32[64,3,4,512]{3,2,1,0:T(4,128)} async-done(((f32[64,3,4,512]{3,2,1,0:T(4,128)}), f32[64,3,4,512]{3,2,1,0:T(4,128)}, u32[]{:S(2)}, u32[]{:S(2)}) %all-to-all-start.5) | async-done | bytes 1572896 | tf_op jit(solution)/shard_map/all_to_all | solution.py:26
  194.5 9.1 %all-to-all-start.4 = ((bf16[64,3,4,512]{3,2,1,0:T(4,128)(2,1)}), bf16[64,3,4,512]{3,2,1,0:T(4,128)(2,1)}, u32[]{:S(2)}, u32[]{:S(2)}) async-start(bf16[64,3,4,512]{3,2,1,0:T(4,128)(2,1)} %broadcast_in_dim.8), calls=%async_computation.4 | async-start | bytes 1572864 | tf_op jit(solution)/shard_map/all_to_all | solution.py:38
  207.0 17.2 %all-to-all-done.4 = bf16[64,3,4,512]{3,2,1,0:T(4,128)(2,1)} async-done(((bf16[64,3,4,512]{3,2,1,0:T(4,128)(2,1)}), bf16[64,3,4,512]{3,2,1,0:T(4,128)(2,1)}, u32[]{:S(2)}, u32[]{:S(2)}) %all-to-all-start.4) | async-done | bytes 786464 | tf_op jit(solution)/shard_map/all_to_all | solution.py:38
  225.3 8.9 %all-to-all-start.6 = ((bf16[64,3,4,512]{3,2,1,0:T(4,128)(2,1)}), bf16[64,3,4,512]{3,2,1,0:T(4,128)(2,1)}, u32[]{:S(2)}, u32[]{:S(2)}) async-start(bf16[64,3,4,512]{3,2,1,0:T(4,128)(2,1)} %broadcast_in_dim.9), calls=%async_computation.6 | async-start | bytes 1572864 | tf_op jit(solution)/shard_map/all_to_all | solution.py:38
  241.2 13.2 %all-to-all-done.6 = bf16[64,3,4,512]{3,2,1,0:T(4,128)(2,1)} async-done(((bf16[64,3,4,512]{3,2,1,0:T(4,128)(2,1)}), bf16[64,3,4,512]{3,2,1,0:T(4,128)(2,1)}, u32[]{:S(2)}, u32[]{:S(2)}) %all-to-all-start.6) | async-done | bytes 786464 | tf_op jit(solution)/shard_map/all_to_all | solution.py:38
  269.2 10.1 %all-to-all-start.7 = ((bf16[4,2,49152]{2,1,0:T(2,128)(2,1)}), bf16[4,2,49152]{2,1,0:T(2,128)(2,1)}, u32[]{:S(2)}, u32[]{:S(2)}) async-start(bf16[4,2,49152]{2,1,0:T(2,128)(2,1)} %reshape.150), calls=%async_computation.7 | async-start | bytes 1572864 | tf_op jit(solution)/shard_map/all_to_all | solution.py:97
  310.4 30.9 %all_to_all.136 = bf16[4,128,3,12,64]{1,0,4,2,3:T(4,128)(2,1)S(1)} all-to-all(bf16[4,128,3,12,64]{1,0,4,2,3:T(4,128)(2,1)S(1)} %copy.130), channel_id=1, replica_groups=mesh['rows'=64,'heads_0'=2,'heads_1'=2] {'heads_0','heads_1'}, dimensions={3} | all-to-all | bytes 4718592 | tf_op jit(solution)/shard_map/all_to_all | solution.py:95
  356.7 6.1 %all-to-all-start.9 = ((f32[64,3,4,512]{3,2,1,0:T(4,128)}), f32[64,3,4,512]{3,2,1,0:T(4,128)}, u32[]{:S(2)}, u32[]{:S(2)}) async-start(f32[64,3,4,512]{3,2,1,0:T(4,128)} %bitcast.149), calls=%async_computation.9 | async-start | bytes 3145728 | tf_op jit(solution)/shard_map/all_to_all | solution.py:26
  369.9 31.0 %all-to-all-done.9 = f32[64,3,4,512]{3,2,1,0:T(4,128)} async-done(((f32[64,3,4,512]{3,2,1,0:T(4,128)}), f32[64,3,4,512]{3,2,1,0:T(4,128)}, u32[]{:S(2)}, u32[]{:S(2)}) %all-to-all-start.9) | async-done | bytes 1572896 | tf_op jit(solution)/shard_map/all_to_all | solution.py:26
  400.9 8.8 %all-to-all-start.11 = ((f32[64,3,4,512]{3,2,1,0:T(4,128)}), f32[64,3,4,512]{3,2,1,0:T(4,128)}, u32[]{:S(2)}, u32[]{:S(2)}) async-start(f32[64,3,4,512]{3,2,1,0:T(4,128)} %bitcast.147), calls=%async_computation.11 | async-start | bytes 3145728 | tf_op jit(solution)/shard_map/all_to_all | solution.py:26
  411.6 35.5 %all-to-all-done.11 = f32[64,3,4,512]{3,2,1,0:T(4,128)} async-done(((f32[64,3,4,512]{3,2,1,0:T(4,128)}), f32[64,3,4,512]{3,2,1,0:T(4,128)}, u32[]{:S(2)}, u32[]{:S(2)}) %all-to-all-start.11) | async-done | bytes 1572896 | tf_op jit(solution)/shard_map/all_to_all | solution.py:26
  448.2 8.9 %all-to-all-start.10 = ((bf16[64,3,4,512]{3,2,1,0:T(4,128)(2,1)}), bf16[64,3,4,512]{3,2,1,0:T(4,128)(2,1)S(1)}, u32[]{:S(2)}, u32[]{:S(2)}) async-start(bf16[64,3,4,512]{3,2,1,0:T(4,128)(2,1)} %broadcast_in_dim.10), calls=%async_computation.10 | async-start | bytes 1572864 | tf_op jit(solution)/shard_map/all_to_all | solution.py:38
  459.0 18.8 %all-to-all-done.10 = bf16[64,3,4,512]{3,2,1,0:T(4,128)(2,1)S(1)} async-done(((bf16[64,3,4,512]{3,2,1,0:T(4,128)(2,1)}), bf16[64,3,4,512]{3,2,1,0:T(4,128)(2,1)S(1)}, u32[]{:S(2)}, u32[]{:S(2)}) %all-to-all-start.10) | async-done | bytes 786464 | tf_op jit(solution)/shard_map/all_to_all | solution.py:38
  478.9 8.9 %all-to-all-start.12 = ((bf16[64,3,4,512]{3,2,1,0:T(4,128)(2,1)}), bf16[64,3,4,512]{3,2,1,0:T(4,128)(2,1)}, u32[]{:S(2)}, u32[]{:S(2)}) async-start(bf16[64,3,4,512]{3,2,1,0:T(4,128)(2,1)} %broadcast_in_dim.11), calls=%async_computation.12 | async-start | bytes 1572864 | tf_op jit(solution)/shard_map/all_to_all | solution.py:38
  490.9 17.1 %all-to-all-done.12 = bf16[64,3,4,512]{3,2,1,0:T(4,128)(2,1)} async-done(((bf16[64,3,4,512]{3,2,1,0:T(4,128)(2,1)}), bf16[64,3,4,512]{3,2,1,0:T(4,128)(2,1)}, u32[]{:S(2)}, u32[]{:S(2)}) %all-to-all-start.12) | async-done | bytes 786464 | tf_op jit(solution)/shard_map/all_to_all | solution.py:38
  514.8 18.7 %all_to_all.137 = bf16[4,2,49152]{2,1,0:T(2,128)(2,1)S(1)} all-to-all(bf16[4,2,49152]{2,1,0:T(2,128)(2,1)S(1)} %reshape.152), channel_id=1, replica_groups=mesh['rows'=64,'heads_0'=2,'heads_1'=2] {'heads_0','heads_1'}, dimensions={0} | all-to-all | bytes 1572864 | tf_op jit(solution)/shard_map/all_to_all | solution.py:97
  539.2 14.0 %all_to_all.138 = bf16[4,128,768]{1,0,2:T(4,128)(2,1)S(1)} all-to-all(bf16[4,128,768]{1,0,2:T(4,128)(2,1)S(1)} %copy.141), channel_id=1, replica_groups=mesh['rows'=64,'heads_0'=2,'heads_1'=2] {'heads_0','heads_1'}, dimensions={2} | all-to-all | bytes 1572864 | tf_op jit(solution)/shard_map/all_to_all | solution.py:109
  (99 shorter events, 162.1 us)
Async XLA Ops:
  10.0 15.7 %all-to-all-start.1 = ((bf16[2,2,4,128,192]{3,4,2,1,0:T(8,128)(2,1)}), bf16[2,2,4,128,192]{3,4,2,1,0:T(8,128)(2,1)}, u32[]{:S(2)}, u32[]{:S(2)}) async-start(bf16[2,2,4,128,192]{3,4,2,1,0:T(8,128)(2,1)} %copy.111), calls=%async_computation.1 | async-start | bytes 1572864 | tf_op jit(solution)/shard_map/all_to_all | solution.py:51
  87.2 0.9 copy-start.1
  96.3 50.8 %all-to-all-start.3 = ((f32[64,3,4,512]{3,2,1,0:T(4,128)}), f32[64,3,4,512]{3,2,1,0:T(4,128)}, u32[]{:S(2)}, u32[]{:S(2)}) async-start(f32[64,3,4,512]{3,2,1,0:T(4,128)} %bitcast.148), calls=%async_computation.3 | async-start | bytes 3145728 | tf_op jit(solution)/shard_map/all_to_all | solution.py:26
  147.2 46.3 %all-to-all-start.5 = ((f32[64,3,4,512]{3,2,1,0:T(4,128)}), f32[64,3,4,512]{3,2,1,0:T(4,128)}, u32[]{:S(2)}, u32[]{:S(2)}) async-start(f32[64,3,4,512]{3,2,1,0:T(4,128)} %bitcast.146), calls=%async_computation.5 | async-start | bytes 3145728 | tf_op jit(solution)/shard_map/all_to_all | solution.py:26
  194.5 29.7 %all-to-all-start.4 = ((bf16[64,3,4,512]{3,2,1,0:T(4,128)(2,1)}), bf16[64,3,4,512]{3,2,1,0:T(4,128)(2,1)}, u32[]{:S(2)}, u32[]{:S(2)}) async-start(bf16[64,3,4,512]{3,2,1,0:T(4,128)(2,1)} %broadcast_in_dim.8), calls=%async_computation.4 | async-start | bytes 1572864 | tf_op jit(solution)/shard_map/all_to_all | solution.py:38
  225.3 29.1 %all-to-all-start.6 = ((bf16[64,3,4,512]{3,2,1,0:T(4,128)(2,1)}), bf16[64,3,4,512]{3,2,1,0:T(4,128)(2,1)}, u32[]{:S(2)}, u32[]{:S(2)}) async-start(bf16[64,3,4,512]{3,2,1,0:T(4,128)(2,1)} %broadcast_in_dim.9), calls=%async_computation.6 | async-start | bytes 1572864 | tf_op jit(solution)/shard_map/all_to_all | solution.py:38
  259.0 1.8 copy-start.4
  269.2 20.8 %all-to-all-start.7 = ((bf16[4,2,49152]{2,1,0:T(2,128)(2,1)}), bf16[4,2,49152]{2,1,0:T(2,128)(2,1)}, u32[]{:S(2)}, u32[]{:S(2)}) async-start(bf16[4,2,49152]{2,1,0:T(2,128)(2,1)} %reshape.150), calls=%async_computation.7 | async-start | bytes 1572864 | tf_op jit(solution)/shard_map/all_to_all | solution.py:97
  279.3 3.7 copy-start.5
  295.1 3.7 copy-start
  297.9 0.9 copy-start.2
  356.7 44.1 %all-to-all-start.9 = ((f32[64,3,4,512]{3,2,1,0:T(4,128)}), f32[64,3,4,512]{3,2,1,0:T(4,128)}, u32[]{:S(2)}, u32[]{:S(2)}) async-start(f32[64,3,4,512]{3,2,1,0:T(4,128)} %bitcast.149), calls=%async_computation.9 | async-start | bytes 3145728 | tf_op jit(solution)/shard_map/all_to_all | solution.py:26
  400.9 46.2 %all-to-all-start.11 = ((f32[64,3,4,512]{3,2,1,0:T(4,128)}), f32[64,3,4,512]{3,2,1,0:T(4,128)}, u32[]{:S(2)}, u32[]{:S(2)}) async-start(f32[64,3,4,512]{3,2,1,0:T(4,128)} %bitcast.147), calls=%async_computation.11 | async-start | bytes 3145728 | tf_op jit(solution)/shard_map/all_to_all | solution.py:26
  448.2 29.6 %all-to-all-start.10 = ((bf16[64,3,4,512]{3,2,1,0:T(4,128)(2,1)}), bf16[64,3,4,512]{3,2,1,0:T(4,128)(2,1)S(1)}, u32[]{:S(2)}, u32[]{:S(2)}) async-start(bf16[64,3,4,512]{3,2,1,0:T(4,128)(2,1)} %broadcast_in_dim.10), calls=%async_computation.10 | async-start | bytes 1572864 | tf_op jit(solution)/shard_map/all_to_all | solution.py:38
  478.9 29.1 %all-to-all-start.12 = ((bf16[64,3,4,512]{3,2,1,0:T(4,128)(2,1)}), bf16[64,3,4,512]{3,2,1,0:T(4,128)(2,1)}, u32[]{:S(2)}, u32[]{:S(2)}) async-start(bf16[64,3,4,512]{3,2,1,0:T(4,128)(2,1)} %broadcast_in_dim.11), calls=%async_computation.12 | async-start | bytes 1572864 | tf_op jit(solution)/shard_map/all_to_all | solution.py:38
  534.7 1.5 copy-start.3
where the time goes:
time: 566 us; the launch traced here: 555 us
  waiting for transfers between devices  201 us (36%)
  local copies, waits for them, and re-layouts  122 us (22%)
  blocking collectives  102 us (18%)
  starting transfers between devices  86.8 us (15%)
  matrix products  28.7 us (5%)
  other arithmetic  13.2 us (2%)
    all_to_all x4, waiting for transfers between devices, sent_and_summed(): lax.all_to_all(pieces, axis, split_axis=0, concat_axis=0, tiled=True)  130 us
    all_to_all x4, waiting for transfers between devices, from_everyone(): lax.all_to_all(jnp.broadcast_to(shard[None], (peers, *shard.shape)), axis...  66.2 us
    all_to_all x2, blocking collectives, on_device(): lax.all_to_all(projected, HEADS_AXES, split_axis=3, concat_axis=1, tiled=...  61.8 us
    all_to_all x4, starting transfers between devices, sent_and_summed(): lax.all_to_all(pieces, axis, split_axis=0, concat_axis=0, tiled=True)  36.6 us
    all_to_all x4, starting transfers between devices, from_everyone(): lax.all_to_all(jnp.broadcast_to(shard[None], (peers, *shard.shape)), axis...  35.8 us
    reshape x9, local copies, waits for them, and re-layouts, in_blocks(): shard.reshape(*lengths[:dim], peers, lengths[dim] // peers, *lengths[dim...  23.9 us
    unnamed x18, local copies, waits for them, and re-layouts  20.9 us
    all_to_all x1, blocking collectives, on_device(): lax.all_to_all(attended, HEADS_AXES, split_axis=1, concat_axis=2, tiled=T...  18.7 us
  transfers between devices with their start and end apart: 10, of which 9 were waited for; matrix products, arithmetic and copies ran while one was open for 10% of the time, Pallas kernels for 0%

commit v1 on v0

v1 whole, which is shorter than its diff:
```python
import functools

import jax
import jax.numpy as jnp
from jax import lax
from jax.experimental import pallas as pl
from jax.experimental.pallas import tpu as pltpu
from jax.sharding import Mesh
from jax.sharding import PartitionSpec as P

D = 768
HEADS = 12
HEAD_DIM = 64
LAYERS = 2
EPSILON = 1e-06
MESH = pl.DeviceIdType.MESH
AXES = ("y", "xh", "z", "xl", "core")
NX, NY, NZ = 4, 4, 8
RES = 512
CORE_HEADS = HEADS // 2
CORE_COLS = CORE_HEADS * HEAD_DIM
QUARTER = D // 4
f32, bf16 = jnp.float32, jnp.bfloat16

RIGHT, LEFT = 0, 1
LONG, SHORT = 0, 1


def wrap(value, n):
    return lax.rem(value + 2 * n, n)


def remote(src, dst, send_sem, recv_sem, device):
    return pltpu.make_async_remote_copy(
        src_ref=src, dst_ref=dst, send_sem=send_sem, recv_sem=recv_sem, device_id=device, device_id_type=MESH
    )


class Ring:
    def __init__(self, n, pos, right, left, send_sems, recv_sems):
        self.n, self.pos, self.devices = n, pos, (right, left)
        self.send_sems, self.recv_sems = send_sems, recv_sems

    def hops(self, kind):
        return self.n // 2 - kind

    def half(self, direction, kind):
        return direction ^ kind

    def index(self, direction, kind, hop):
        return direction * (self.n - 1) + kind * (self.n // 2) + hop - 1

    def owner(self, direction, distance):
        return wrap(self.pos + (distance if direction == RIGHT else -distance), self.n)

    def copy(self, src, dst, direction, i):
        return remote(src, dst, self.send_sems.at[i], self.recv_sems.at[i], self.devices[direction])

    def each(self):
        for kind in (LONG, SHORT):
            for direction in (RIGHT, LEFT):
                yield direction, kind

    def scatter_start(self, view, slot):
        for direction, kind in self.each():
            i = self.index(direction, kind, 1)
            self.copy(
                view(self.owner(direction, self.hops(kind)), self.half(direction, kind)), slot(i), direction, i
            ).start()

    def scatter_event(self, view, slot, kind, hop):
        for direction in (RIGHT, LEFT):
            i = self.index(direction, kind, hop)
            self.copy(slot(i), slot(i), direction, i).wait_recv()
            if hop < self.hops(kind):
                own = view(self.owner(direction, self.hops(kind) - hop), self.half(direction, kind))
                slot(i)[...] = slot(i)[...] + own[...]
                self.copy(slot(i), slot(i + 1), direction, i + 1).start()

    def scatter_result(self, view, slot, half):
        total = view(self.pos, half)[...]
        for direction, kind in self.each():
            if self.half(direction, kind) == half:
                total = total + slot(self.index(direction, kind, self.hops(kind)))[...]
        return total

    def scatter_sent(self, slot):
        for direction, kind in self.each():
            for hop in range(1, self.hops(kind) + 1):
                i = self.index(direction, kind, hop)
                self.copy(slot(i), slot(i), direction, i).wait_send()

    def gather_start(self, view):
        for direction, kind in self.each():
            i = self.index(direction, kind, 1)
            block = view(self.pos, self.half(direction, kind))
            self.copy(block, block, direction, i).start()

    def gather_event(self, view, kind, hop):
        for direction in (RIGHT, LEFT):
            i = self.index(direction, kind, hop)
            block = view(self.owner(direction, -hop), self.half(direction, kind))
            self.copy(block, block, direction, i).wait_recv()
            if hop < self.hops(kind):
                self.copy(block, block, direction, i + 1).start()

    def gather_sent(self, view):
        for direction, kind in self.each():
            block = view(self.pos, self.half(direction, kind))
            for hop in range(1, self.hops(kind) + 1):
                i = self.index(direction, kind, hop)
                self.copy(block, block, direction, i).wait_send()

    def events(self):
        for hop in range(1, self.n // 2 + 1):
            for kind in (LONG, SHORT):
                if hop <= self.hops(kind):
                    yield kind, hop


class Direct:
    def __init__(self, peers, pos, send_sems, recv_sems):
        self.peers, self.pos = peers, pos
        self.send_sems, self.recv_sems = send_sems, recv_sems

    def copy(self, src, dst, k):
        return remote(src, dst, self.send_sems.at[k], self.recv_sems.at[k], self.peers[k][0])

    def scatter_start(self, blocks, slots):
        for k, (_, index) in enumerate(self.peers):
            self.copy(blocks.at[index], slots.at[k], k).start()

    def scatter_result(self, blocks, slots):
        for k in range(len(self.peers)):
            self.copy(slots.at[k], slots.at[k], k).wait_recv()
        total = blocks[self.pos]
        for k in range(len(self.peers)):
            total = total + slots[k]
        return total

    def gather_start(self, blocks):
        for k in range(len(self.peers)):
            self.copy(blocks.at[self.pos], blocks.at[self.pos], k).start()

    def arrived(self, blocks):
        for k in range(len(self.peers)):
            self.copy(blocks.at[self.pos], blocks.at[self.pos], k).wait_recv()

    def sent(self, blocks):
        for k in range(len(self.peers)):
            self.copy(blocks.at[self.pos], blocks.at[self.pos], k).wait_send()


def softmax(scores, scale):
    shifted = (scores - jnp.max(scores, axis=-1, keepdims=True)) * scale
    grown = jnp.exp(shifted)
    return (grown / jnp.sum(grown, axis=-1, keepdims=True)).astype(bf16)


def whole(
    scale, tok, wqkv, wo, gain, out,
    x, wq_in, wo_in, wq_t, wo_t, gain_t, qkv, att,
    s_a, s_b, s_c, r_a, r_b, r_c, acc_a, acc_b, acc_c, r_b2, r_c2, acc_b2, acc_c2, d_a, d_b, d_c,
    w_a, w_b, w_c, g_a, g_b, g_c,
    ss_a, rs_a, ss_b, rs_b, ss_c, rs_c, ss_b2, rs_b2, ss_c2, rs_c2, ss_da, rs_da, ss_db, rs_db, ss_dc, rs_dc,
    sg_a, rg_a, sg_b, rg_b, sg_c, rg_c, sg_b2, rg_b2, sg_c2, rg_c2, sg_da, rg_da, sg_db, rg_db, sg_dc, rg_dc,
    w_sems, x_local, x_send, x_recv, f_send, f_recv, t_send, t_recv, o_local, o_send, o_recv,
):
    y, xh, z = lax.axis_index("y"), lax.axis_index("xh"), lax.axis_index("z")
    xl, core = lax.axis_index("xl"), lax.axis_index("core")
    xpos = xh * 2 + xl

    def at_x(p):
        return {"xh": lax.div(p, 2), "xl": lax.rem(p, 2)}

    x_right, x_left = at_x(wrap(xpos + 1, NX)), at_x(wrap(xpos - 1, NX))
    y_right, y_left = {"y": wrap(y + 1, NY)}, {"y": wrap(y - 1, NY)}
    z_right, z_left = {"z": wrap(z + 1, NZ)}, {"z": wrap(z - 1, NZ)}
    plane = []
    for dx in range(NX):
        for dy in range(NY):
            if dx or dy:
                px, py = wrap(xpos + dx, NX), wrap(y + dy, NY)
                plane.append(({**at_x(px), "y": py}, px * NY + py))
    along_z = [({"z": wrap(z + dz, NZ)}, wrap(z + dz, NZ)) for dz in range(1, NZ)]
    other_core = {"core": 1 - core}
    partner = {"xl": 1 - xl}

    loads = []
    for layer in range(LAYERS):
        for t in range(3):
            loads.append(
                pltpu.make_async_copy(
                    wqkv.at[layer, t, :, pl.ds(pl.multiple_of(core * CORE_COLS, 128), CORE_COLS)],
                    wq_in.at[layer, t],
                    w_sems.at[layer * 4 + t],
                )
            )
        loads.append(pltpu.make_async_copy(wo.at[layer], wo_in.at[layer], w_sems.at[layer * 4 + 3]))
    own_quarter, far_quarter = 2 * xl + core, 2 * (1 - xl) + core
    near_pair, far_pair = 2 * xl, 2 * (1 - xl)

    def quarter(q, offset, size):
        return pl.ds(pl.multiple_of(q * QUARTER + offset, 32), size)

    own_tokens = pltpu.make_async_copy(tok.at[pl.ds(near_pair, 2)], x.at[:, quarter(own_quarter, 0, QUARTER)], x_local)
    own_tokens.start()
    for load in loads:
        load.start()

    barrier = pltpu.get_barrier_semaphore()
    partners = [device for device, _ in plane + along_z] + [other_core]
    for device in partners:
        pl.semaphore_signal(barrier, inc=1, device_id=device, device_id_type=MESH)
    pl.semaphore_wait(barrier, len(partners))

    half_quarter = QUARTER // 2
    pieces = [(s, f) for s in range(2) for f in range(2)]

    def piece(q, s, f):
        return x.at[s, quarter(q, f * half_quarter, half_quarter)]

    for k, (s, f) in enumerate(pieces):
        remote(
            tok.at[far_pair + s, pl.ds(f * half_quarter, half_quarter)], piece(own_quarter, s, f),
            x_send.at[k], x_recv.at[k], partner,
        ).start()
    remote(
        tok.at[pl.ds(near_pair, 2)], x.at[:, quarter(own_quarter, 0, QUARTER)], f_send.at[4], f_recv.at[4], other_core
    ).start()

    for load in loads:
        load.wait()

    def turn(layer, carry):
        for t in range(3):
            wq_t[layer, t] = wq_in[layer, t].T
        for m in range(3):
            wo_t[layer, m * 256 : (m + 1) * 256] = wo_in[layer, :, m * 256 : (m + 1) * 256].T
        return carry

    lax.fori_loop(0, LAYERS, turn, 0)
    for layer in range(LAYERS):
        row = gain[layer : layer + 1, :].astype(f32)
        gain_t[layer] = jnp.broadcast_to(row, (128, D)).T

    for k, (s, f) in enumerate(pieces):
        arrived = piece(far_quarter, s, f)
        remote(arrived, arrived, x_send.at[k], x_recv.at[k], partner).wait_recv()
        remote(arrived, arrived, f_send.at[k], f_recv.at[k], other_core).start()
    own_tokens.wait()
    near = x.at[:, quarter(2 * xl + 1 - core, 0, QUARTER)]
    remote(near, near, f_send.at[4], f_recv.at[4], other_core).wait_recv()
    for k, (s, f) in enumerate(pieces):
        arrived = piece(2 * (1 - xl) + 1 - core, s, f)
        remote(arrived, arrived, f_send.at[k], f_recv.at[k], other_core).wait_recv()
    for k, (s, f) in enumerate(pieces):
        block = piece(far_quarter, s, f)
        remote(block, block, x_send.at[k], x_recv.at[k], partner).wait_send()
        remote(block, block, f_send.at[k], f_recv.at[k], other_core).wait_send()
    near = x.at[:, quarter(own_quarter, 0, QUARTER)]
    remote(near, near, f_send.at[4], f_recv.at[4], other_core).wait_send()

    ring_a = Ring(NZ, z, z_right, z_left, ss_a, rs_a)
    ring_b = Ring(NY, y, y_right, y_left, ss_b, rs_b)
    ring_c = Ring(NX, xpos, x_right, x_left, ss_c, rs_c)
    ring_b2 = Ring(NX, xpos, x_right, x_left, ss_b2, rs_b2)
    ring_c2 = Ring(NY, y, y_right, y_left, ss_c2, rs_c2)
    plane_pos = xpos * NY + y
    direct_a = Direct(plane, plane_pos, ss_da, rs_da)
    direct_b = Direct(along_z, z, ss_db, rs_db)
    direct_c = Direct(along_z, z, ss_dc, rs_dc)
    back_a = Ring(NZ, z, z_right, z_left, sg_a, rg_a)
    back_b = Ring(NY, y, y_right, y_left, sg_b, rg_b)
    back_c = Ring(NX, xpos, x_right, x_left, sg_c, rg_c)
    back_b2 = Ring(NX, xpos, x_right, x_left, sg_b2, rg_b2)
    back_c2 = Ring(NY, y, y_right, y_left, sg_c2, rg_c2)
    spread_a = Direct(plane, plane_pos, sg_da, rg_da)
    spread_b = Direct(along_z, z, sg_db, rg_db)
    spread_c = Direct(along_z, z, sg_dc, rg_dc)

    def pairs(ref):
        return lambda owner, half: ref.at[2 * owner + half]

    def fours(ref):
        return lambda owner, half: ref.at[owner, pl.ds(4 * half, 4)]

    def slots(ref):
        return lambda i: ref.at[i]

    def layer_step(layer, carry):
        def project(t, carry):
            for s in range(2):
                columns = jnp.dot(wq_t[layer, t], x[s], preferred_element_type=f32)
                qkv[t, :, s * HEAD_DIM : (s + 1) * HEAD_DIM, :] = columns.astype(bf16).reshape(
                    CORE_HEADS, HEAD_DIM, RES
                )
            return carry

        lax.fori_loop(0, 3, project, 0)

        def score(first, store):
            def body(h, carry):
                store(
                    h,
                    lax.dot_general(
                        qkv[0, first + h].T, qkv[1, first + h], (((1,), (0,)), ((), ())), preferred_element_type=f32
                    ),
                )
                return carry

            lax.fori_loop(0, 2, body, 0)

        def store_a(h, value):
            s_a[pl.ds(h * 8, 8)] = value.reshape(8, 64, RES)

        def store_b(h, value):
            s_b[pl.ds(h * 2, 2)] = value.reshape(2, 8, 32, RES)

        def store_c(h, value):
            s_c[pl.ds(h * 2, 2)] = value.reshape(2, 8, 32, RES)

        score(0, store_a)
        ring_a.scatter_start(pairs(s_a), slots(r_a))
        score(2, store_b)
        ring_b.scatter_start(fours(s_b), slots(r_b))
        score(4, store_c)
        ring_c.scatter_start(fours(s_c), slots(r_c))

        def step_a(kind, hop):
            ring_a.scatter_event(pairs(s_a), slots(r_a), kind, hop)

        def step_bc(kind, hop):
            ring_b.scatter_event(fours(s_b), slots(r_b), kind, hop)
            ring_c.scatter_event(fours(s_c), slots(r_c), kind, hop)

        def step_bc2(kind, hop):
            ring_b2.scatter_event(pairs(acc_b), slots(r_b2), kind, hop)
            ring_c2.scatter_event(pairs(acc_c), slots(r_c2), kind, hop)

        step_a(LONG, 1)
        step_bc(LONG, 1)
        step_a(SHORT, 1)
        step_a(LONG, 2)
        step_bc(SHORT, 1)
        step_a(SHORT, 2)
        step_a(LONG, 3)
        step_bc(LONG, 2)
        for half in range(2):
            acc_b[4 * half : 4 * half + 4] = ring_b.scatter_result(fours(s_b), slots(r_b), half)
            acc_c[4 * half : 4 * half + 4] = ring_c.scatter_result(fours(s_c), slots(r_c), half)
        ring_b2.scatter_start(pairs(acc_b), slots(r_b2))
        ring_c2.scatter_start(pairs(acc_c), slots(r_c2))
        step_a(SHORT, 3)
        step_bc2(LONG, 1)
        step_a(LONG, 4)
        for half in range(2):
            acc_a[8 * half : 8 * half + 8] = ring_a.scatter_result(pairs(s_a), slots(r_a), half).reshape(8, 8, RES)
        direct_a.scatter_start(acc_a, d_a)
        step_bc2(SHORT, 1)
        step_bc2(LONG, 2)
        for half in range(2):
            acc_b2[4 * half : 4 * half + 4] = ring_b2.scatter_result(pairs(acc_b), slots(r_b2), half).reshape(4, 8, RES)
            acc_c2[4 * half : 4 * half + 4] = ring_c2.scatter_result(pairs(acc_c), slots(r_c2), half).reshape(4, 8, RES)
        direct_b.scatter_start(acc_b2, d_b)
        direct_c.scatter_start(acc_c2, d_c)

        g_a[plane_pos] = softmax(direct_a.scatter_result(acc_a, d_a), scale)
        spread_a.gather_start(g_a)
        g_b[z] = softmax(direct_b.scatter_result(acc_b2, d_b), scale)
        spread_b.gather_start(g_b)
        g_c[z] = softmax(direct_c.scatter_result(acc_c2, d_c), scale)
        ring_a.scatter_sent(slots(r_a))
        ring_b.scatter_sent(slots(r_b))
        ring_c.scatter_sent(slots(r_c))
        ring_b2.scatter_sent(slots(r_b2))
        ring_c2.scatter_sent(slots(r_c2))
        spread_c.gather_start(g_c)

        def joined(ref, first, blocks):
            return ref[first : first + blocks].astype(f32).reshape(blocks * 8, RES).astype(bf16)

        spread_a.arrived(g_a)
        for half in range(2):
            w_a[2 * z + half] = joined(g_a, 8 * half, 8)
        back_a.gather_start(pairs(w_a))
        spread_b.arrived(g_b)
        spread_c.arrived(g_c)
        for half in range(2):
            w_b[y, 2 * xpos + half] = joined(g_b, 4 * half, 4)
            w_c[xpos, 2 * y + half] = joined(g_c, 4 * half, 4)
        view_b2 = lambda owner, half: w_b.at[y, 2 * owner + half]
        view_c2 = lambda owner, half: w_c.at[xpos, 2 * owner + half]
        back_b2.gather_start(view_b2)
        back_c2.gather_start(view_c2)

        def back_bc2(kind, hop):
            back_b2.gather_event(view_b2, kind, hop)
            back_c2.gather_event(view_c2, kind, hop)

        def back_bc(kind, hop):
            back_b.gather_event(fours(w_b), kind, hop)
            back_c.gather_event(fours(w_c), kind, hop)

        back_a.gather_event(pairs(w_a), LONG, 1)
        back_bc2(LONG, 1)
        back_bc2(SHORT, 1)
        back_a.gather_event(pairs(w_a), SHORT, 1)
        back_bc2(LONG, 2)
        back_b.gather_start(fours(w_b))
        back_c.gather_start(fours(w_c))
        back_a.gather_event(pairs(w_a), LONG, 2)
        back_a.gather_event(pairs(w_a), SHORT, 2)
        back_bc(LONG, 1)
        back_a.gather_event(pairs(w_a), LONG, 3)
        back_a.gather_event(pairs(w_a), SHORT, 3)
        back_bc(SHORT, 1)
        back_a.gather_event(pairs(w_a), LONG, 4)

        def attend(first, load):
            def body(h, carry):
                heads = lax.dot_general(
                    qkv[2, first + h], load(h), (((1,), (1,)), ((), ())), preferred_element_type=f32
                ).astype(bf16)
                for s in range(2):
                    at = pl.ds(pl.multiple_of((first + h) * HEAD_DIM, HEAD_DIM), HEAD_DIM)
                    att[layer, s, core, at, :] = heads[s * HEAD_DIM : (s + 1) * HEAD_DIM]
                return carry

            lax.fori_loop(0, 2, body, 0)

        def trade(colour, owner):
            return remote(
                att.at[layer, :, owner, pl.ds(128 * colour, 128)], att.at[layer, :, owner, pl.ds(128 * colour, 128)],
                t_send.at[colour], t_recv.at[layer, colour], other_core,
            )

        attend(0, lambda h: w_a[pl.ds(h * 8, 8)].reshape(RES, RES))
        trade(0, core).start()
        back_bc(LONG, 2)
        attend(2, lambda h: w_b[pl.ds(h * 2, 2)].reshape(RES, RES))
        trade(1, core).start()
        attend(4, lambda h: w_c[pl.ds(h * 2, 2)].reshape(RES, RES))
        trade(2, core).start()

        direct_a.sent(acc_a)
        direct_b.sent(acc_b2)
        direct_c.sent(acc_c2)
        spread_a.sent(g_a)
        spread_b.sent(g_b)
        spread_c.sent(g_c)
        back_a.gather_sent(pairs(w_a))
        back_b.gather_sent(fours(w_b))
        back_c.gather_sent(fours(w_c))
        back_b2.gather_sent(view_b2)
        back_c2.gather_sent(view_c2)

        for colour in range(3):
            trade(colour, 1 - core).wait_recv()
        for colour in range(3):
            trade(colour, core).wait_send()

        def finish(step, carry):
            s = lax.div(step, 2)
            at = pl.ds(pl.multiple_of(lax.rem(step, 2) * 256, 256), 256)
            heads = att[layer, s, :, :, at].reshape(D, 256)
            update = jnp.dot(wo_t[layer], heads, preferred_element_type=f32)
            summed = x[s, :, at].astype(f32) + update
            mean_sq = jnp.mean(summed * summed, axis=0, keepdims=True)
            gains = gain_t[layer]
            normed = summed * lax.rsqrt(mean_sq + EPSILON) * jnp.concatenate([gains, gains], axis=1)
            x[s, :, at] = normed.astype(bf16)
            return carry

        lax.fori_loop(0, 4, finish, 0)
        return carry

    lax.fori_loop(0, LAYERS, layer_step, 0)

    own_out = pltpu.make_async_copy(x.at[:, quarter(own_quarter, 0, QUARTER)], out.at[pl.ds(near_pair, 2)], o_local)
    far_out = remote(
        x.at[:, quarter(far_quarter, 0, QUARTER)], out.at[pl.ds(near_pair, 2)], o_send.at[0], o_recv.at[0], partner
    )
    far_out.start()
    own_out.start()
    own_out.wait()
    far_out.wait_send()
    landed = out.at[pl.ds(far_pair, 2)]
    remote(landed, landed, o_send.at[0], o_recv.at[0], partner).wait_recv()


def on_device(tokens, qkv_weight, out_weight, norm_gain):
    scale = 1.0 / (HEAD_DIM * 2 * NX * NY * NZ) ** 0.5
    any_space = pl.BlockSpec(memory_space=pl.ANY)
    vmem = pl.BlockSpec(memory_space=pltpu.VMEM)
    dma = pltpu.SemaphoreType.DMA
    ring = lambda n: 2 * (n - 1)
    counts = [ring(NZ), ring(NY), ring(NX), ring(NX), ring(NY), NX * NY - 1, NZ - 1, NZ - 1]
    sems = [dma((count,)) for count in counts for _ in range(2)]
    result = pl.pallas_call(
        functools.partial(whole, scale),
        out_shape=jax.ShapeDtypeStruct((4, QUARTER, RES), bf16),
        in_specs=[any_space, any_space, any_space, vmem],
        out_specs=any_space,
        scratch_shapes=[
            pltpu.VMEM((2, D, RES), bf16),
            pltpu.VMEM((LAYERS, 3, D, CORE_COLS), bf16),
            pltpu.VMEM((LAYERS, D, D), bf16),
            pltpu.VMEM((LAYERS, 3, CORE_COLS, D), bf16),
            pltpu.VMEM((LAYERS, D, D), bf16),
            pltpu.VMEM((LAYERS, D, 128), f32),
            pltpu.VMEM((3, CORE_HEADS, 2 * HEAD_DIM, RES), bf16),
            pltpu.VMEM((LAYERS, 2, 2, CORE_COLS, RES), bf16),
            pltpu.VMEM((16, 64, RES), f32),
            pltpu.VMEM((4, 8, 32, RES), f32),
            pltpu.VMEM((4, 8, 32, RES), f32),
            pltpu.VMEM((14, 64, RES), f32),
            pltpu.VMEM((6, 4, 32, RES), f32),
            pltpu.VMEM((6, 4, 32, RES), f32),
            pltpu.VMEM((16, 8, RES), f32),
            pltpu.VMEM((8, 32, RES), f32),
            pltpu.VMEM((8, 32, RES), f32),
            pltpu.VMEM((6, 32, RES), f32),
            pltpu.VMEM((6, 32, RES), f32),
            pltpu.VMEM((8, 8, RES), f32),
            pltpu.VMEM((8, 8, RES), f32),
            pltpu.VMEM((15, 8, RES), f32),
            pltpu.VMEM((7, 8, RES), f32),
            pltpu.VMEM((7, 8, RES), f32),
            pltpu.VMEM((16, 64, RES), bf16),
            pltpu.VMEM((4, 8, 32, RES), bf16),
            pltpu.VMEM((4, 8, 32, RES), bf16),
            pltpu.VMEM((16, 8, RES), bf16),
            pltpu.VMEM((8, 8, RES), bf16),
            pltpu.VMEM((8, 8, RES), bf16),
            *sems,
            *sems,
            dma((4 * LAYERS,)),
            dma,
            dma((4,)),
            dma((4,)),
            dma((5,)),
            dma((5,)),
            dma((3,)),
            dma((LAYERS, 3)),
            dma,
            dma((1,)),
            dma((1,)),
        ],
        compiler_params=pltpu.CompilerParams(
            collective_id=0, has_side_effects=True, vmem_limit_bytes=60 * 1024 * 1024
        ),
    )(
        tokens.transpose(0, 2, 1),
        qkv_weight.transpose(0, 2, 1, 3),
        out_weight,
        norm_gain,
    )
    return result.transpose(0, 2, 1)


def solution(mesh):
    finer = Mesh(mesh.devices.reshape(NY, NX // 2, NZ, 2, 2), AXES)
    rows, heads = ("y", "xh", "z"), ("xl", "core")
    return jax.shard_map(
        on_device,
        mesh=finer,
        in_specs=(P(rows, None, heads), P(), P(), P()),
        out_specs=P(rows, None, heads),
        check_vma=False,
    )
```

time: 566 us -> 175 us (0.31); the launches traced: 555 us -> 175 us
  waiting for transfers between devices: 201 us -> 0 us
  Pallas kernels: 0 us -> 172 us
  local copies, waits for them, and re-layouts: 122 us -> 2.06 us
  blocking collectives: 102 us -> 0 us
  starting transfers between devices: 86.8 us -> 0 us
  matrix products: 28.7 us -> 0 us
  other arithmetic: 13.2 us -> 0 us
    all_to_all x10 -> x0, waiting for transfers between devices: 201 us -> none  [the longest x4 130 us: sent_and_summed(): lax.all_to_all(pieces, axis, split_axis=0, concat_axis=0, tiled=True)]
    pallas_call x0 -> x1, Pallas kernels: none -> 172 us  [on_device(): pl.pallas_call(functools.partial(whole, scale), out_shape=jax.ShapeDtypeS...]
    all_to_all x5 -> x0, blocking collectives: 102 us -> none  [the longest x2 61.8 us: on_device(): lax.all_to_all(projected, HEADS_AXES, split_axis=3, concat_axis=1, tiled=...]
    all_to_all x10 -> x0, starting transfers between devices: 86.8 us -> none  [the longest x4 36.6 us: sent_and_summed(): lax.all_to_all(pieces, axis, split_axis=0, concat_axis=0, tiled=True)]
    reshape x18 -> x0, local copies, waits for them, and re-layouts: 44.9 us -> none  [the longest x9 23.9 us: in_blocks(): shard.reshape(*lengths[:dim], peers, lengths[dim] // peers, *lengths[dim...]
    dot_general x12 -> x0, matrix products: 28.7 us -> none  [the longest x2 8.94 us: on_device(): jnp.dot(stream.reshape(seq_dev * quarter, D), qkv_matrix, preferred_eleme...]
    all_to_all x11 -> x0, local copies, waits for them, and re-layouts: 23.5 us -> none  [the longest x6 17.7 us: on_device(): lax.all_to_all(projected, HEADS_AXES, split_axis=3, concat_axis=1, tiled=...]
    unnamed x18 -> x1, local copies, waits for them, and re-layouts: 20.9 us -> 2.06 us
  transfers between devices with their start and end apart: 10 -> 0, of which waited for: 9 -> 0; matrix products, arithmetic and copies ran while one was open for 10% -> 0% of each run, Pallas kernels for 0% -> 0%
where the time goes in v1:
time: 175 us
  Pallas kernels  172 us (98%)
  local copies, waits for them, and re-layouts  2.06 us (1%)
    pallas_call x1, Pallas kernels, on_device(): pl.pallas_call(functools.partial(whole, scale), out_shape=jax.ShapeDtypeS...  172 us

profile of v1, /device:TPU:1, one launch (start us, length us, event | category | flops | bytes accessed | tf_op | source)
XLA Modules:
  0.0 174.6 jit_solution(14703880839741682304)
XLA Ops:
  0.0 172.5 %shard_map.46 = bf16[4,192,512]{2,1,0:T(8,128)(2,1)} custom-call(bf16[4,192,512]{2,1,0:T(8,128)(2,1)} %bitcast.5, bf16[2,3,768,768]{3,2,1,0:T(8,128)(2,1)} %bitcast.3, bf16[2,768,768]{2,1,0:T(8,128)(2,1)} %wo.1, bf16[2,768]{1,0:T(2,128)(2,1)} %gain.1), custom_call_target="tpu_custom_call" | custom-call | tf_op jit(solution)/shard_map/pallas_call | solution.py:500
  172.5 2.1 %copy.6 = bf16[4,512,192]{1,2,0:T(8,128)(2,1)} copy(bf16[4,512,192]{1,2,0:T(8,128)(2,1)} %bitcast.4) | data formatting | bytes 1572864

commit v2 on v0

v2 whole, which is shorter than its diff:
```python
import functools

import jax
import jax.numpy as jnp
from jax import lax
from jax.experimental import pallas as pl
from jax.experimental.pallas import tpu as pltpu
from jax.sharding import Mesh
from jax.sharding import PartitionSpec as P

D = 768
HEADS = 12
HEAD_DIM = 64
LAYERS = 2
EPSILON = 1e-06
MESH = pl.DeviceIdType.MESH
AXES = ("y", "xh", "z", "xl", "core")
NX, NY, NZ = 4, 4, 8
RES = 512
BLOCK = RES // 2
CORE_HEADS = HEADS // 2
CORE_COLS = CORE_HEADS * HEAD_DIM
QUARTER = D // 4
f32, bf16 = jnp.float32, jnp.bfloat16

RIGHT, LEFT = 0, 1
LONG, SHORT = 0, 1


def wrap(value, n):
    return lax.rem(value + 2 * n, n)


def remote(src, dst, send_sem, recv_sem, device):
    return pltpu.make_async_remote_copy(
        src_ref=src, dst_ref=dst, send_sem=send_sem, recv_sem=recv_sem, device_id=device, device_id_type=MESH
    )


class Clock:
    RATE, FIRST_HOP, NEXT_HOP = 54e3, 2.2, 0.63

    def __init__(self):
        self.now, self.free = 0.0, {}

    def spend(self, time):
        self.now += time

    def send(self, link, size, hops=1):
        begin = max(self.now, self.free.get(link, 0.0))
        self.free[link] = begin + size / self.RATE
        return self.free[link] + self.FIRST_HOP + self.NEXT_HOP * (hops - 1)


class Ring:
    def __init__(self, clock, axis, size, n, pos, right, left, send_sems, recv_sems):
        self.clock, self.axis, self.size = clock, axis, size
        self.n, self.pos, self.devices = n, pos, (right, left)
        self.send_sems, self.recv_sems = send_sems, recv_sems
        self.due = {}

    def hops(self, kind):
        return self.n // 2 - kind

    def half(self, direction, kind):
        return direction ^ kind

    def index(self, direction, kind, hop):
        return direction * (self.n - 1) + kind * (self.n // 2) + hop - 1

    def owner(self, direction, distance):
        return wrap(self.pos + (distance if direction == RIGHT else -distance), self.n)

    def copy(self, src, dst, direction, i):
        return remote(src, dst, self.send_sems(i), self.recv_sems(i), self.devices[direction])

    def start(self, src, dst, direction, kind, hop):
        self.copy(src, dst, direction, self.index(direction, kind, hop)).start()
        self.due[kind, hop] = self.clock.send((self.axis, direction), self.size)

    def each(self):
        for kind in (LONG, SHORT):
            for direction in (RIGHT, LEFT):
                yield direction, kind

    def events(self):
        for hop in range(1, self.n // 2 + 1):
            for kind in (LONG, SHORT):
                if hop <= self.hops(kind):
                    yield kind, hop

    def scatter(self, view, slot, after_first=None):
        for direction, kind in self.each():
            own = view(self.owner(direction, self.hops(kind)), self.half(direction, kind))
            self.start(own, slot(self.index(direction, kind, 1)), direction, kind, 1)
        for kind, hop in self.events():
            yield self.due[kind, hop]
            for direction in (RIGHT, LEFT):
                i = self.index(direction, kind, hop)
                self.copy(slot(i), slot(i), direction, i).wait_recv()
                if hop < self.hops(kind):
                    own = view(self.owner(direction, self.hops(kind) - hop), self.half(direction, kind))
                    slot(i)[...] = slot(i)[...] + own[...]
                    self.start(slot(i), slot(i + 1), direction, kind, hop + 1)
            self.clock.spend(self.size / 500e3)
            if after_first is not None and (kind, hop) == (LONG, 1):
                after_first()

    def scatter_result(self, view, slot, half):
        total = view(self.pos, half)[...]
        for direction, kind in self.each():
            if self.half(direction, kind) == half:
                total = total + slot(self.index(direction, kind, self.hops(kind)))[...]
        return total

    def scatter_sent(self, slot):
        for direction, kind in self.each():
            for hop in range(1, self.hops(kind) + 1):
                i = self.index(direction, kind, hop)
                self.copy(slot(i), slot(i), direction, i).wait_send()

    def gather(self, view):
        for direction, kind in self.each():
            block = view(self.pos, self.half(direction, kind))
            self.start(block, block, direction, kind, 1)
        for kind, hop in self.events():
            yield self.due[kind, hop]
            for direction in (RIGHT, LEFT):
                i = self.index(direction, kind, hop)
                block = view(self.owner(direction, -hop), self.half(direction, kind))
                self.copy(block, block, direction, i).wait_recv()
                if hop < self.hops(kind):
                    self.start(block, block, direction, kind, hop + 1)

    def gather_sent(self, view):
        for direction, kind in self.each():
            block = view(self.pos, self.half(direction, kind))
            for hop in range(1, self.hops(kind) + 1):
                i = self.index(direction, kind, hop)
                self.copy(block, block, direction, i).wait_send()


class Direct:
    def __init__(self, clock, size, peers, pos, owns, send_sems, recv_sems):
        self.clock, self.size, self.peers, self.pos, self.owns = clock, size, peers, pos, owns
        self.send_sems, self.recv_sems = send_sems, recv_sems

    def copy(self, src, dst, k):
        return remote(src, dst, self.send_sems(k), self.recv_sems(k), self.peers[k][0])

    def to_owners(self, action):
        same = [k for k, peer in enumerate(self.peers) if peer[2]]
        other = [k for k, peer in enumerate(self.peers) if not peer[2]]

        @pl.when(self.owns)
        def _():
            for k in same:
                action(k)

        @pl.when(jnp.logical_not(self.owns))
        def _():
            for k in other:
                action(k)

    def price(self, count):
        return max(
            self.clock.send(link, self.size * count / len(self.peers), hops) for _, _, _, link, hops in self.peers
        )

    def scatter_start(self, blocks, slots):
        self.to_owners(lambda k: self.copy(blocks.at[self.peers[k][1]], slots(k), k).start())
        return self.price(len(self.peers) // 2)

    def turn(self, blocks, slots, spread, weights, scale):
        every = range(len(self.peers))

        @pl.when(self.owns)
        def _():
            for k in every:
                self.copy(slots(k), slots(k), k).wait_recv()
            total = blocks[self.pos]
            for k in every:
                total = total + slots(k)[...]
            weights[self.pos] = softmax(total, scale)
            for k in every:
                spread.copy(weights.at[self.pos], weights.at[self.pos], k).start()

        self.clock.spend(0.6)
        return spread.price(len(self.peers) // 2)

    def arrived(self, blocks):
        self.to_owners(lambda k: self.copy(blocks.at[self.pos], blocks.at[self.pos], k).wait_recv())

    def scatter_sent(self, blocks):
        self.to_owners(lambda k: self.copy(blocks.at[self.pos], blocks.at[self.pos], k).wait_send())

    def gather_sent(self, blocks):
        @pl.when(self.owns)
        def _():
            for k in range(len(self.peers)):
                self.copy(blocks.at[self.pos], blocks.at[self.pos], k).wait_send()


def softmax(scores, scale):
    shifted = (scores - jnp.max(scores, axis=-1, keepdims=True)) * scale
    grown = jnp.exp(shifted)
    return (grown / jnp.sum(grown, axis=-1, keepdims=True)).astype(bf16)


def whole(
    scale, tok, wqkv, wo, gain, out,
    x, wq_in, wo_in, wq_t, wo_t, gain_t, qkv, att,
    s_a, s_b, s_c, r_a, r_b, r_c, acc_a, acc_b, acc_c, r_b2, r_c2, acc_b2, acc_c2, d_a, d_b, d_c,
    w_a, w_b, w_c, g_a, g_b, g_c, ring_sems, direct_sems,
    w_sems, x_local, x_send, x_recv, f_send, f_recv, t_send, t_recv, o_local, o_send, o_recv,
):
    y, xh, z = lax.axis_index("y"), lax.axis_index("xh"), lax.axis_index("z")
    xl, core = lax.axis_index("xl"), lax.axis_index("core")
    xpos = xh * 2 + xl

    def at_x(p):
        return {"xh": lax.div(p, 2), "xl": lax.rem(p, 2)}

    x_right, x_left = at_x(wrap(xpos + 1, NX)), at_x(wrap(xpos - 1, NX))
    y_right, y_left = {"y": wrap(y + 1, NY)}, {"y": wrap(y - 1, NY)}
    z_right, z_left = {"z": wrap(z + 1, NZ)}, {"z": wrap(z - 1, NZ)}
    plane = []
    for dx in range(NX):
        for dy in range(NY):
            if dx or dy:
                px, py = wrap(xpos + dx, NX), wrap(y + dy, NY)
                link = ("x", int(dx > NX // 2)) if dx else ("y", int(dy > NY // 2))
                far = min(dx, NX - dx) + min(dy, NY - dy)
                index = px * (NY // 2) + lax.div(py, 2)
                plane.append(({**at_x(px), "y": py}, index, (dx + dy) % 2 == 0, link, far))
    along_z = []
    for dz in range(1, NZ):
        pz = wrap(z + dz, NZ)
        along_z.append(({"z": pz}, lax.div(pz, 2), dz % 2 == 0, ("z", int(dz > NZ // 2)), min(dz, NZ - dz)))
    other_core = {"core": 1 - core}
    partner = {"xl": 1 - xl}

    loads = []
    for layer in range(LAYERS):
        for t in range(3):
            loads.append(
                pltpu.make_async_copy(
                    wqkv.at[layer, t, :, pl.ds(pl.multiple_of(core * CORE_COLS, 128), CORE_COLS)],
                    wq_in.at[layer, t],
                    w_sems.at[layer * 4 + t],
                )
            )
        loads.append(pltpu.make_async_copy(wo.at[layer], wo_in.at[layer], w_sems.at[layer * 4 + 3]))
    own_quarter, far_quarter = 2 * xl + core, 2 * (1 - xl) + core
    near_pair, far_pair = 2 * xl, 2 * (1 - xl)

    def quarter(q):
        return pl.ds(pl.multiple_of(q * QUARTER, 64), QUARTER)

    own_tokens = pltpu.make_async_copy(tok.at[pl.ds(near_pair, 2)], x.at[:, quarter(own_quarter)], x_local)
    own_tokens.start()
    for load in loads:
        load.start()

    barrier = pltpu.get_barrier_semaphore()
    partners = [peer[0] for peer in plane + along_z] + [other_core]
    for device in partners:
        pl.semaphore_signal(barrier, inc=1, device_id=device, device_id_type=MESH)
    pl.semaphore_wait(barrier, len(partners))

    def block(b):
        return slice(b * BLOCK, (b + 1) * BLOCK)

    pieces = [(b, s) for b in range(2) for s in range(2)]

    def piece(q, b, s):
        return x.at[s, quarter(q), block(b)]

    for k, (b, s) in enumerate(pieces):
        remote(
            tok.at[far_pair + s, :, block(b)], piece(own_quarter, b, s), x_send.at[k], x_recv.at[k], partner
        ).start()
    remote(
        tok.at[pl.ds(near_pair, 2)], x.at[:, quarter(own_quarter)], f_send.at[4], f_recv.at[4], other_core
    ).start()

    def turn_columns(layer, t):
        loads[layer * 4 + t].wait()
        wq_t[layer, t] = wq_in[layer, t].T

    def turn_out(layer):
        loads[layer * 4 + 3].wait()
        for m in range(3):
            wo_t[layer, m * 256 : (m + 1) * 256] = wo_in[layer, :, m * 256 : (m + 1) * 256].T
        row = gain[layer : layer + 1, :].astype(f32)
        gain_t[layer] = jnp.broadcast_to(row, (128, D)).T

    clock = Clock()

    def project(layer, t, b):
        for s in range(2):
            columns = jnp.dot(wq_t[layer, t], x[s, :, block(b)], preferred_element_type=f32)
            qkv[layer, t, :, s * HEAD_DIM : (s + 1) * HEAD_DIM, block(b)] = columns.astype(bf16).reshape(
                CORE_HEADS, HEAD_DIM, BLOCK
            )
        clock.spend(0.5)

    turn_columns(0, 0)
    turn_columns(0, 1)
    for k, (b, s) in enumerate(pieces):
        arrived = piece(far_quarter, b, s)
        remote(arrived, arrived, x_send.at[k], x_recv.at[k], partner).wait_recv()
        remote(arrived, arrived, f_send.at[k], f_recv.at[k], other_core).start()
        if k == 0:
            turn_columns(0, 2)
            own_tokens.wait()
            near = x.at[:, quarter(2 * xl + 1 - core)]
            remote(near, near, f_send.at[4], f_recv.at[4], other_core).wait_recv()
        if k == 2:
            for j in range(2):
                arrived = piece(2 * (1 - xl) + 1 - core, *pieces[j])
                remote(arrived, arrived, f_send.at[j], f_recv.at[j], other_core).wait_recv()
            project(0, 0, 0)
            project(0, 1, 0)
    for j in range(2, 4):
        arrived = piece(2 * (1 - xl) + 1 - core, *pieces[j])
        remote(arrived, arrived, f_send.at[j], f_recv.at[j], other_core).wait_recv()
    project(0, 0, 1)
    project(0, 1, 1)

    def tokens_sent():
        for k, (b, s) in enumerate(pieces):
            arrived = piece(far_quarter, b, s)
            remote(arrived, arrived, x_send.at[k], x_recv.at[k], partner).wait_send()
            remote(arrived, arrived, f_send.at[k], f_recv.at[k], other_core).wait_send()
        near = x.at[:, quarter(own_quarter)]
        remote(near, near, f_send.at[4], f_recv.at[4], other_core).wait_send()

    plane_pos = xpos * (NY // 2) + lax.div(y, 2)
    z_pos = lax.div(z, 2)
    plane_parity, z_parity = lax.rem(xpos + y, 2), lax.rem(z, 2)

    def taker(table):
        taken = [0]

        def take(count):
            first = taken[0]
            taken[0] += count
            return lambda i: table.at[first + i]

        return take

    row = RES * 4

    def colour_rings(b):
        take_ring, take_direct = taker(ring_sems.at[b]), taker(direct_sems.at[b])

        def ring(axis, rows, width):
            n, pos, right, left = {
                "x": (NX, xpos, x_right, x_left),
                "y": (NY, y, y_right, y_left),
                "z": (NZ, z, z_right, z_left),
            }[axis]
            count = 2 * (n - 1)
            return Ring(clock, axis, rows * row * width, n, pos, right, left, take_ring(count), take_ring(count))

        def direct(peers, width):
            pos, parity = (plane_pos, plane_parity) if peers is plane else (z_pos, z_parity)
            return Direct(
                clock, 8 * row * width, peers, pos, parity == b, take_direct(len(peers)), take_direct(len(peers))
            )

        return [
            dict(
                down=[ring("z", 32, 1)], owners=direct(plane, 1), spread=direct(plane, 0.5), up=[ring("z", 32, 0.5)]
            )
        ] + [
            dict(
                down=[ring(first, 64, 1), ring(second, 16, 1)],
                owners=direct(along_z, 1),
                spread=direct(along_z, 0.5),
                up=[ring(second, 16, 0.5), ring(first, 64, 0.5)],
            )
            for first, second in (("y", "x"), ("x", "y"))
        ]

    groups = [colour_rings(b) for b in range(2)]

    def slots(ref, b):
        return lambda i: ref.at[b, i]

    def pairs(ref, b):
        return lambda owner, half: ref.at[b, 2 * owner + half]

    def fours(ref, b):
        return lambda owner, half: ref.at[b, owner, pl.ds(4 * half, 4)]

    places = [
        dict(s=s_a, r=r_a, r2=None, acc=None, last=acc_a, d=d_a, w=w_a, g=g_a, view=pairs, blocks=(8, 32)),
        dict(s=s_b, r=r_b, r2=r_b2, acc=acc_b, last=acc_b2, d=d_b, w=w_b, g=g_b, view=fours, blocks=(2, 8, 16)),
        dict(s=s_c, r=r_c, r2=r_c2, acc=acc_c, last=acc_c2, d=d_c, w=w_c, g=g_c, view=fours, blocks=(2, 8, 16)),
    ]
    middle = [None, lambda b: lambda owner, half: w_b.at[b, y, 2 * owner + half],
              lambda b: lambda owner, half: w_c.at[b, xpos, 2 * owner + half]]

    def trade(layer, b, colour, owner):
        part = att.at[layer, :, owner, pl.ds(128 * colour, 128), block(b)]
        return remote(part, part, t_send.at[b, colour], t_recv.at[layer, b, colour], other_core)

    def score(layer, b, colour):
        place = places[colour]
        blocks = place["blocks"]

        def body(h, carry):
            head = 2 * colour + h
            scores = jnp.dot(
                qkv[layer, 0, head, :, block(b)].T, qkv[layer, 1, head], preferred_element_type=f32
            )
            place["s"][b, pl.ds(h * blocks[0], blocks[0])] = scores.reshape(*blocks, RES)
            return carry

        lax.fori_loop(0, 2, body, 0)
        clock.spend(0.5)

    def attend(layer, b, colour):
        place = places[colour]
        blocks = place["blocks"]

        def body(h, carry):
            head = 2 * colour + h
            weights = place["w"][b, pl.ds(h * blocks[0], blocks[0])].reshape(BLOCK, RES)
            heads = lax.dot_general(
                qkv[layer, 2, head], weights, (((1,), (1,)), ((), ())), preferred_element_type=f32
            ).astype(bf16)
            at = pl.ds(pl.multiple_of(head * HEAD_DIM, HEAD_DIM), HEAD_DIM)
            for s in range(2):
                att[layer, s, core, at, block(b)] = heads[s * HEAD_DIM : (s + 1) * HEAD_DIM]
            return carry

        lax.fori_loop(0, 2, body, 0)
        clock.spend(0.6)

    def joined(ref, b, first, blocks):
        return ref[b, first : first + blocks].astype(f32).reshape(blocks * 8, RES).astype(bf16)

    def colour_steps(layer, b, colour, after_first, done):
        place, group = places[colour], groups[b][colour]
        view, slot = place["view"](place["s"], b), slots(place["r"], b)
        score(layer, b, colour)
        down = group["down"]
        yield from down[0].scatter(view, slot, after_first)
        last = place["last"].at[b]
        if colour == 0:
            for half in range(2):
                last[4 * half : 4 * half + 4] = down[0].scatter_result(view, slot, half).reshape(4, 8, RES)
        else:
            view2, slot2 = pairs(place["acc"], b), slots(place["r2"], b)
            for half in range(2):
                place["acc"][b, 4 * half : 4 * half + 4] = down[0].scatter_result(view, slot, half)
            yield from down[1].scatter(view2, slot2)
            for half in range(2):
                last[2 * half : 2 * half + 2] = down[1].scatter_result(view2, slot2, half).reshape(2, 8, RES)
            down[1].scatter_sent(slot2)
        down[0].scatter_sent(slot)
        yield group["owners"].scatter_start(last, slots(place["d"], b))
        yield group["owners"].turn(last, slots(place["d"], b), group["spread"], place["g"].at[b], scale)
        group["spread"].arrived(place["g"].at[b])
        w, up = place["w"], group["up"]
        if colour == 0:
            for half in range(2):
                w[b, 2 * z + half] = joined(place["g"], b, 4 * half, 4)
        else:
            first, second = (y, xpos) if colour == 1 else (xpos, y)
            for half in range(2):
                w[b, first, 2 * second + half] = joined(place["g"], b, 2 * half, 2)
            yield from up[0].gather(middle[colour](b))
        yield from up[-1].gather(place["view"](w, b))
        attend(layer, b, colour)
        trade(layer, b, colour, core).start()
        done()

    def all_sent(b):
        for colour in range(3):
            place, group = places[colour], groups[b][colour]
            group["owners"].scatter_sent(place["last"].at[b])
            group["spread"].gather_sent(place["g"].at[b])
            group["up"][-1].gather_sent(place["view"](place["w"], b))
            if colour:
                group["up"][0].gather_sent(middle[colour](b))

    def finish(layer, b):
        def body(s, carry):
            heads = att[layer, s, :, :, block(b)].reshape(D, BLOCK)
            update = jnp.dot(wo_t[layer], heads, preferred_element_type=f32)
            summed = x[s, :, block(b)].astype(f32) + update
            mean_sq = jnp.mean(summed * summed, axis=0, keepdims=True)
            gains = gain_t[layer]
            normed = summed * lax.rsqrt(mean_sq + EPSILON) * jnp.concatenate([gains, gains], axis=1)
            x[s, :, block(b)] = normed.astype(bf16)
            return carry

        lax.fori_loop(0, 2, body, 0)
        clock.spend(1.5)

    def far_out(b):
        return remote(
            x.at[:, quarter(far_quarter), block(b)], out.at[pl.ds(near_pair, 2), :, block(b)],
            o_send.at[b], o_recv.at[b], partner,
        )

    def own_out(b):
        return pltpu.make_async_copy(
            x.at[:, quarter(own_quarter), block(b)], out.at[pl.ds(near_pair, 2), :, block(b)], o_local.at[b]
        )

    def finish_steps(layer, b):
        yield clock.now + 1.6
        for colour in range(3):
            trade(layer, b, colour, 1 - core).wait_recv()
        finish(layer, b)
        if layer + 1 < LAYERS:
            project(layer + 1, 0, b)
            project(layer + 1, 1, b)
        else:
            far_out(b).start()
            own_out(b).start()

    for layer in range(LAYERS):
        running, order = [], [0]

        def add(steps, running=running, order=order):
            due = next(steps, None)
            if due is not None:
                order[0] += 1
                running.append((due, order[0], steps))

        def launch(b, colour, layer=layer, add=add):
            left[b][colour] = 1

            def after_first():
                if b == 0:
                    launch(1, colour)

            def done():
                left[b][colour] = 0
                if sum(left[b].values()) == 0 and len(left[b]) == 3:
                    add(finish_steps(layer, b))

            add(colour_steps(layer, b, colour, after_first, done))

        left = [{}, {}]
        for colour in range(3):
            launch(0, colour)
        for b in range(2):
            project(layer, 2, b)
        fillers = []
        if layer == 0:
            tokens_sent()
            fillers = [functools.partial(turn_out, 0)]
            fillers += [functools.partial(turn_columns, 1, t) for t in range(3)]
            fillers += [functools.partial(turn_out, 1)]
        while running:
            running.sort(key=lambda entry: entry[:2])
            if fillers and running[0][0] > clock.now + 0.7:
                fillers.pop(0)()
                clock.spend(1.0)
                continue
            due, _, steps = running.pop(0)
            clock.now = max(clock.now, due)
            add(steps)
        for filler in fillers:
            filler()
        for b in range(2):
            all_sent(b)
            for colour in range(3):
                trade(layer, b, colour, core).wait_send()

    for b in range(2):
        own_out(b).wait()
        far_out(b).wait_send()
        landed = out.at[pl.ds(far_pair, 2), :, block(b)]
        remote(landed, landed, o_send.at[b], o_recv.at[b], partner).wait_recv()


def on_device(tokens, qkv_weight, out_weight, norm_gain):
    scale = 1.0 / (HEAD_DIM * 2 * NX * NY * NZ) ** 0.5
    any_space = pl.BlockSpec(memory_space=pl.ANY)
    vmem = pl.BlockSpec(memory_space=pltpu.VMEM)
    dma = pltpu.SemaphoreType.DMA
    around = lambda n: 2 * (n - 1)
    ring_count = 4 * (around(NZ) + 2 * around(NX) + 2 * around(NY))
    direct_count = 4 * (NX * NY - 1 + 2 * (NZ - 1))
    result = pl.pallas_call(
        functools.partial(whole, scale),
        out_shape=jax.ShapeDtypeStruct((4, QUARTER, RES), bf16),
        in_specs=[any_space, any_space, any_space, vmem],
        out_specs=vmem,
        scratch_shapes=[
            pltpu.VMEM((2, D, RES), bf16),
            pltpu.VMEM((LAYERS, 3, D, CORE_COLS), bf16),
            pltpu.VMEM((LAYERS, D, D), bf16),
            pltpu.VMEM((LAYERS, 3, CORE_COLS, D), bf16),
            pltpu.VMEM((LAYERS, D, D), bf16),
            pltpu.VMEM((LAYERS, D, 128), f32),
            pltpu.VMEM((LAYERS, 3, CORE_HEADS, 2 * HEAD_DIM, RES), bf16),
            pltpu.VMEM((LAYERS, 2, 2, CORE_COLS, RES), bf16),
            pltpu.VMEM((2, 16, 32, RES), f32),
            pltpu.VMEM((2, 4, 8, 16, RES), f32),
            pltpu.VMEM((2, 4, 8, 16, RES), f32),
            pltpu.VMEM((2, 14, 32, RES), f32),
            pltpu.VMEM((2, 6, 4, 16, RES), f32),
            pltpu.VMEM((2, 6, 4, 16, RES), f32),
            pltpu.VMEM((2, 8, 8, RES), f32),
            pltpu.VMEM((2, 8, 16, RES), f32),
            pltpu.VMEM((2, 8, 16, RES), f32),
            pltpu.VMEM((2, 6, 16, RES), f32),
            pltpu.VMEM((2, 6, 16, RES), f32),
            pltpu.VMEM((2, 4, 8, RES), f32),
            pltpu.VMEM((2, 4, 8, RES), f32),
            pltpu.VMEM((2, 15, 8, RES), f32),
            pltpu.VMEM((2, 7, 8, RES), f32),
            pltpu.VMEM((2, 7, 8, RES), f32),
            pltpu.VMEM((2, 16, 32, RES), bf16),
            pltpu.VMEM((2, 4, 8, 16, RES), bf16),
            pltpu.VMEM((2, 4, 8, 16, RES), bf16),
            pltpu.VMEM((2, 8, 8, RES), bf16),
            pltpu.VMEM((2, 4, 8, RES), bf16),
            pltpu.VMEM((2, 4, 8, RES), bf16),
            dma((2, ring_count)),
            dma((2, direct_count)),
            dma((4 * LAYERS,)),
            dma,
            dma((4,)),
            dma((4,)),
            dma((5,)),
            dma((5,)),
            dma((2, 3)),
            dma((LAYERS, 2, 3)),
            dma((2,)),
            dma((2,)),
            dma((2,)),
        ],
        compiler_params=pltpu.CompilerParams(
            collective_id=0, has_side_effects=True, vmem_limit_bytes=60 * 1024 * 1024
        ),
    )(
        tokens.transpose(0, 2, 1),
        qkv_weight.transpose(0, 2, 1, 3),
        out_weight,
        norm_gain,
    )
    return result.transpose(0, 2, 1)


def solution(mesh):
    finer = Mesh(mesh.devices.reshape(NY, NX // 2, NZ, 2, 2), AXES)
    rows, heads = ("y", "xh", "z"), ("xl", "core")
    return jax.shard_map(
        on_device,
        mesh=finer,
        in_specs=(P(rows, None, heads), P(), P(), P()),
        out_specs=P(rows, None, heads),
        check_vma=False,
    )
```

time: 566 us -> 165 us (0.29); the launches traced: 555 us -> 165 us
  waiting for transfers between devices: 201 us -> 0 us
  Pallas kernels: 0 us -> 163 us
  local copies, waits for them, and re-layouts: 122 us -> 2.06 us
  blocking collectives: 102 us -> 0 us
  starting transfers between devices: 86.8 us -> 0 us
  matrix products: 28.7 us -> 0 us
  other arithmetic: 13.2 us -> 0 us
    all_to_all x10 -> x0, waiting for transfers between devices: 201 us -> none  [the longest x4 130 us: sent_and_summed(): lax.all_to_all(pieces, axis, split_axis=0, concat_axis=0, tiled=True)]
    pallas_call x0 -> x1, Pallas kernels: none -> 163 us  [on_device(): pl.pallas_call(functools.partial(whole, scale), out_shape=jax.ShapeDtypeS...]
    all_to_all x5 -> x0, blocking collectives: 102 us -> none  [the longest x2 61.8 us: on_device(): lax.all_to_all(projected, HEADS_AXES, split_axis=3, concat_axis=1, tiled=...]
    all_to_all x10 -> x0, starting transfers between devices: 86.8 us -> none  [the longest x4 36.6 us: sent_and_summed(): lax.all_to_all(pieces, axis, split_axis=0, concat_axis=0, tiled=True)]
    reshape x18 -> x0, local copies, waits for them, and re-layouts: 44.9 us -> none  [the longest x9 23.9 us: in_blocks(): shard.reshape(*lengths[:dim], peers, lengths[dim] // peers, *lengths[dim...]
    dot_general x12 -> x0, matrix products: 28.7 us -> none  [the longest x2 8.94 us: on_device(): jnp.dot(stream.reshape(seq_dev * quarter, D), qkv_matrix, preferred_eleme...]
    all_to_all x11 -> x0, local copies, waits for them, and re-layouts: 23.5 us -> none  [the longest x6 17.7 us: on_device(): lax.all_to_all(projected, HEADS_AXES, split_axis=3, concat_axis=1, tiled=...]
    unnamed x18 -> x1, local copies, waits for them, and re-layouts: 20.9 us -> 2.06 us
  transfers between devices with their start and end apart: 10 -> 0, of which waited for: 9 -> 0; matrix products, arithmetic and copies ran while one was open for 10% -> 0% of each run, Pallas kernels for 0% -> 0%
where the time goes in v2:
time: 165 us
  Pallas kernels  163 us (99%)
  local copies, waits for them, and re-layouts  2.06 us (1%)
    pallas_call x1, Pallas kernels, on_device(): pl.pallas_call(functools.partial(whole, scale), out_shape=jax.ShapeDtypeS...  163 us

profile of v2, /device:TPU:1, one launch (start us, length us, event | category | flops | bytes accessed | tf_op | source)
XLA Modules:
  0.0 164.8 jit_solution(1374442909522839120)
XLA Ops:
  0.0 162.7 %shard_map.46 = bf16[4,192,512]{2,1,0:T(8,128)(2,1)} custom-call(bf16[4,192,512]{2,1,0:T(8,128)(2,1)} %bitcast.5, bf16[2,3,768,768]{3,2,1,0:T(8,128)(2,1)} %bitcast.3, bf16[2,768,768]{2,1,0:T(8,128)(2,1)} %wo.1, bf16[2,768]{1,0:T(2,128)(2,1)} %gain.1), custom_call_target="tpu_custom_call" | custom-call | tf_op jit(solution)/shard_map/pallas_call | solution.py:593
  162.7 2.1 %copy.6 = bf16[4,512,192]{1,2,0:T(8,128)(2,1)} copy(bf16[4,512,192]{1,2,0:T(8,128)(2,1)} %bitcast.4) | data formatting | bytes 1572864

commit v3 on v2

--- a/solution.py
+++ b/solution.py
@@ -37,8 +37,39 @@
     )
 
 
+STEPS = 195.0
+LOWEST = 100.0
+
+
+def encode(value):
+    rows, columns = value.shape
+    size = jnp.abs(value)
+    top = functools.reduce(
+        jnp.maximum,
+        [size[r : r + 8, c : c + 128] for r in range(0, rows, 8) for c in range(0, columns, 128)],
+    )
+    top = jnp.maximum(top, 1e-30)
+    per_unit = jnp.concatenate([STEPS / top] * (columns // 128), axis=1)
+    per_unit = jnp.concatenate([per_unit] * (rows // 8), axis=0)
+    level = size * per_unit
+    binade = jnp.floor(level)
+    code = (1.0 + (level - binade)) * jnp.exp2(binade - LOWEST)
+    return jnp.where(value < 0, -code, code).astype(bf16), top / STEPS
+
+
+def decode(code, unit):
+    rows, columns = code.shape
+    code = code.astype(f32)
+    size = jnp.abs(code)
+    binade = jnp.floor(jnp.log2(size))
+    level = binade + size * jnp.exp2(-binade) + (LOWEST - 1.0)
+    unit = jnp.concatenate([unit] * (columns // 128), axis=1)
+    unit = jnp.concatenate([unit] * (rows // 8), axis=0)
+    return jnp.where(code < 0, -level, level) * unit
+
+
 class Clock:
-    RATE, FIRST_HOP, NEXT_HOP = 54e3, 2.2, 0.63
+    RATE, FIRST_HOP, NEXT_HOP = 46e3, 2.6, 0.65
 
     def __init__(self):
         self.now, self.free = 0.0, {}
@@ -140,6 +171,61 @@
                 self.copy(block, block, direction, i).wait_send()
 
 
+class CodedRing(Ring):
+    def pair(self, src, dst, direction, i):
+        count = 2 * (self.n - 1)
+        return self.copy(src[0], dst[0], direction, i), self.copy(src[1], dst[1], direction, count + i)
+
+    def start_pair(self, src, dst, direction, kind, hop):
+        for copy in self.pair(src, dst, direction, self.index(direction, kind, hop)):
+            copy.start()
+        self.due[kind, hop] = self.clock.send((self.axis, direction), self.size + 4096)
+
+    @staticmethod
+    def put(place, value):
+        codes, units = encode(value)
+        place[0][...] = codes
+        place[1][...] = units
+
+    @staticmethod
+    def get(place):
+        return decode(place[0][...], place[1][...])
+
+    def scatter(self, view, slot, staged, after_first=None):
+        for direction, kind in self.each():
+            place = staged(direction * 2 + kind)
+            self.put(place, view(self.owner(direction, self.hops(kind)), self.half(direction, kind)))
+            self.start_pair(place, slot(self.index(direction, kind, 1)), direction, kind, 1)
+            self.clock.spend(0.1)
+        for kind, hop in self.events():
+            yield self.due[kind, hop]
+            for direction in (RIGHT, LEFT):
+                i = self.index(direction, kind, hop)
+                for copy in self.pair(slot(i), slot(i), direction, i):
+                    copy.wait_recv()
+                if hop < self.hops(kind):
+                    own = view(self.owner(direction, self.hops(kind) - hop), self.half(direction, kind))
+                    self.put(slot(i), self.get(slot(i)) + own)
+                    self.start_pair(slot(i), slot(i + 1), direction, kind, hop + 1)
+            self.clock.spend(0.4)
+            if after_first is not None and (kind, hop) == (LONG, 1):
+                after_first()
+
+    def scatter_result(self, view, slot, half):
+        total = view(self.pos, half)
+        for direction, kind in self.each():
+            if self.half(direction, kind) == half:
+                total = total + self.get(slot(self.index(direction, kind, self.hops(kind))))
+        return total
+
+    def scatter_sent(self, slot):
+        for direction, kind in self.each():
+            for hop in range(1, self.hops(kind) + 1):
+                i = self.index(direction, kind, hop)
+                for copy in self.pair(slot(i), slot(i), direction, i):
+                    copy.wait_send()
+
+
 class Direct:
     def __init__(self, clock, size, peers, pos, owns, send_sems, recv_sems):
         self.clock, self.size, self.peers, self.pos, self.owns = clock, size, peers, pos, owns
@@ -211,7 +297,7 @@
     scale, tok, wqkv, wo, gain, out,
     x, wq_in, wo_in, wq_t, wo_t, gain_t, qkv, att,
     s_a, s_b, s_c, r_a, r_b, r_c, acc_a, acc_b, acc_c, r_b2, r_c2, acc_b2, acc_c2, d_a, d_b, d_c,
-    w_a, w_b, w_c, g_a, g_b, g_c, ring_sems, direct_sems,
+    w_a, w_b, w_c, g_a, g_b, g_c, e_a, e_b, e_c, ue_a, ue_b, ue_c, ur_a, ur_b, ur_c, ring_sems, direct_sems,
     w_sems, x_local, x_send, x_recv, f_send, f_recv, t_send, t_recv, o_local, o_send, o_recv,
 ):
     y, xh, z = lax.axis_index("y"), lax.axis_index("xh"), lax.axis_index("z")
@@ -355,14 +441,14 @@
     def colour_rings(b):
         take_ring, take_direct = taker(ring_sems.at[b]), taker(direct_sems.at[b])
 
-        def ring(axis, rows, width):
+        def ring(axis, rows, width, kind=Ring):
             n, pos, right, left = {
                 "x": (NX, xpos, x_right, x_left),
                 "y": (NY, y, y_right, y_left),
                 "z": (NZ, z, z_right, z_left),
             }[axis]
-            count = 2 * (n - 1)
-            return Ring(clock, axis, rows * row * width, n, pos, right, left, take_ring(count), take_ring(count))
+            count = 2 * (n - 1) * (2 if kind is CodedRing else 1)
+            return kind(clock, axis, rows * row * width, n, pos, right, left, take_ring(count), take_ring(count))
 
         def direct(peers, width):
             pos, parity = (plane_pos, plane_parity) if peers is plane else (z_pos, z_parity)
@@ -372,11 +458,11 @@
 
         return [
             dict(
-                down=[ring("z", 32, 1)], owners=direct(plane, 1), spread=direct(plane, 0.5), up=[ring("z", 32, 0.5)]
+                down=[ring("z", 32, 0.5, CodedRing)], owners=direct(plane, 1), spread=direct(plane, 0.5), up=[ring("z", 32, 0.5)]
             )
         ] + [
             dict(
-                down=[ring(first, 64, 1), ring(second, 16, 1)],
+                down=[ring(first, 64, 0.5, CodedRing), ring(second, 16, 1)],
                 owners=direct(along_z, 1),
                 spread=direct(along_z, 0.5),
                 up=[ring(second, 16, 0.5), ring(first, 64, 0.5)],
@@ -395,10 +481,16 @@
     def fours(ref, b):
         return lambda owner, half: ref.at[b, owner, pl.ds(4 * half, 4)]
 
+    def coded(codes, units, b):
+        return lambda i: (codes.at[b, i], units.at[b, i])
+
+    def terms(view):
+        return lambda owner, half: view(owner, half)[...].reshape(-1, RES)
+
     places = [
-        dict(s=s_a, r=r_a, r2=None, acc=None, last=acc_a, d=d_a, w=w_a, g=g_a, view=pairs, blocks=(8, 32)),
-        dict(s=s_b, r=r_b, r2=r_b2, acc=acc_b, last=acc_b2, d=d_b, w=w_b, g=g_b, view=fours, blocks=(2, 8, 16)),
-        dict(s=s_c, r=r_c, r2=r_c2, acc=acc_c, last=acc_c2, d=d_c, w=w_c, g=g_c, view=fours, blocks=(2, 8, 16)),
+        dict(s=s_a, r=(r_a, ur_a), e=(e_a, ue_a), r2=None, acc=None, last=acc_a, d=d_a, w=w_a, g=g_a, view=pairs, blocks=(8, 32)),
+        dict(s=s_b, r=(r_b, ur_b), e=(e_b, ue_b), r2=r_b2, acc=acc_b, last=acc_b2, d=d_b, w=w_b, g=g_b, view=fours, blocks=(2, 8, 16)),
+        dict(s=s_c, r=(r_c, ur_c), e=(e_c, ue_c), r2=r_c2, acc=acc_c, last=acc_c2, d=d_c, w=w_c, g=g_c, view=fours, blocks=(2, 8, 16)),
     ]
     middle = [None, lambda b: lambda owner, half: w_b.at[b, y, 2 * owner + half],
               lambda b: lambda owner, half: w_c.at[b, xpos, 2 * owner + half]]
@@ -445,10 +537,10 @@
 
     def colour_steps(layer, b, colour, after_first, done):
         place, group = places[colour], groups[b][colour]
-        view, slot = place["view"](place["s"], b), slots(place["r"], b)
+        view, slot, staged = terms(place["view"](place["s"], b)), coded(*place["r"], b), coded(*place["e"], b)
         score(layer, b, colour)
         down = group["down"]
-        yield from down[0].scatter(view, slot, after_first)
+        yield from down[0].scatter(view, slot, staged, after_first)
         last = place["last"].at[b]
         if colour == 0:
             for half in range(2):
@@ -456,7 +548,7 @@
         else:
             view2, slot2 = pairs(place["acc"], b), slots(place["r2"], b)
             for half in range(2):
-                place["acc"][b, 4 * half : 4 * half + 4] = down[0].scatter_result(view, slot, half)
+                place["acc"][b, 4 * half : 4 * half + 4] = down[0].scatter_result(view, slot, half).reshape(4, 16, RES)
             yield from down[1].scatter(view2, slot2)
             for half in range(2):
                 last[2 * half : 2 * half + 2] = down[1].scatter_result(view2, slot2, half).reshape(2, 8, RES)
@@ -588,13 +680,13 @@
     vmem = pl.BlockSpec(memory_space=pltpu.VMEM)
     dma = pltpu.SemaphoreType.DMA
     around = lambda n: 2 * (n - 1)
-    ring_count = 4 * (around(NZ) + 2 * around(NX) + 2 * around(NY))
+    ring_count = 4 * (around(NZ) + 2 * around(NX) + 2 * around(NY)) + 2 * (around(NZ) + around(NX) + around(NY))
     direct_count = 4 * (NX * NY - 1 + 2 * (NZ - 1))
     result = pl.pallas_call(
         functools.partial(whole, scale),
         out_shape=jax.ShapeDtypeStruct((4, QUARTER, RES), bf16),
         in_specs=[any_space, any_space, any_space, vmem],
-        out_specs=vmem,
+        out_specs=any_space,
         scratch_shapes=[
             pltpu.VMEM((2, D, RES), bf16),
             pltpu.VMEM((LAYERS, 3, D, CORE_COLS), bf16),
@@ -607,9 +699,9 @@
             pltpu.VMEM((2, 16, 32, RES), f32),
             pltpu.VMEM((2, 4, 8, 16, RES), f32),
             pltpu.VMEM((2, 4, 8, 16, RES), f32),
-            pltpu.VMEM((2, 14, 32, RES), f32),
-            pltpu.VMEM((2, 6, 4, 16, RES), f32),
-            pltpu.VMEM((2, 6, 4, 16, RES), f32),
+            pltpu.VMEM((2, 14, 32, RES), bf16),
+            pltpu.VMEM((2, 6, 64, RES), bf16),
+            pltpu.VMEM((2, 6, 64, RES), bf16),
             pltpu.VMEM((2, 8, 8, RES), f32),
             pltpu.VMEM((2, 8, 16, RES), f32),
             pltpu.VMEM((2, 8, 16, RES), f32),
@@ -626,6 +718,15 @@
             pltpu.VMEM((2, 8, 8, RES), bf16),
             pltpu.VMEM((2, 4, 8, RES), bf16),
             pltpu.VMEM((2, 4, 8, RES), bf16),
+            pltpu.VMEM((2, 4, 32, RES), bf16),
+            pltpu.VMEM((2, 4, 64, RES), bf16),
+            pltpu.VMEM((2, 4, 64, RES), bf16),
+            pltpu.VMEM((2, 4, 8, 128), f32),
+            pltpu.VMEM((2, 4, 8, 128), f32),
+            pltpu.VMEM((2, 4, 8, 128), f32),
+            pltpu.VMEM((2, 14, 8, 128), f32),
+            pltpu.VMEM((2, 6, 8, 128), f32),
+            pltpu.VMEM((2, 6, 8, 128), f32),
             dma((2, ring_count)),
             dma((2, direct_count)),
             dma((4 * LAYERS,)),

time: 165 us -> 155 us (0.939)
  Pallas kernels: 163 us -> 153 us
    pallas_call x1, Pallas kernels: 163 us -> 153 us  [on_device(): pl.pallas_call(functools.partial(whole, scale), out_shape=jax.ShapeDtypeS...]
where the time goes in v3:
time: 155 us
  Pallas kernels  153 us (99%)
  local copies, waits for them, and re-layouts  2.06 us (1%)
    pallas_call x1, Pallas kernels, on_device(): pl.pallas_call(functools.partial(whole, scale), out_shape=jax.ShapeDtypeS...  153 us

profile of v3, /device:TPU:1, one launch (start us, length us, event | category | flops | bytes accessed | tf_op | source)
XLA Modules:
  0.0 155.1 jit_solution(7483078520979484931)
XLA Ops:
  0.0 153.0 %shard_map.46 = bf16[4,192,512]{2,1,0:T(8,128)(2,1)} custom-call(bf16[4,192,512]{2,1,0:T(8,128)(2,1)} %bitcast.5, bf16[2,3,768,768]{3,2,1,0:T(8,128)(2,1)} %bitcast.3, bf16[2,768,768]{2,1,0:T(8,128)(2,1)} %wo.1, bf16[2,768]{1,0:T(2,128)(2,1)} %gain.1), custom_call_target="tpu_custom_call" | custom-call | tf_op jit(solution)/shard_map/pallas_call | solution.py:685
  153.0 2.1 %copy.6 = bf16[4,512,192]{1,2,0:T(8,128)(2,1)} copy(bf16[4,512,192]{1,2,0:T(8,128)(2,1)} %bitcast.4) | data formatting | bytes 1572864

commit v4 on v3

--- a/solution.py
+++ b/solution.py
@@ -69,7 +69,7 @@
 
 
 class Clock:
-    RATE, FIRST_HOP, NEXT_HOP = 46e3, 2.6, 0.65
+    RATE, FIRST_HOP, NEXT_HOP = 46e3, 3.0, 0.65
 
     def __init__(self):
         self.now, self.free = 0.0, {}
@@ -120,7 +120,7 @@
                 if hop <= self.hops(kind):
                     yield kind, hop
 
-    def scatter(self, view, slot, after_first=None):
+    def scatter(self, view, slot):
         for direction, kind in self.each():
             own = view(self.owner(direction, self.hops(kind)), self.half(direction, kind))
             self.start(own, slot(self.index(direction, kind, 1)), direction, kind, 1)
@@ -134,8 +134,6 @@
                     slot(i)[...] = slot(i)[...] + own[...]
                     self.start(slot(i), slot(i + 1), direction, kind, hop + 1)
             self.clock.spend(self.size / 500e3)
-            if after_first is not None and (kind, hop) == (LONG, 1):
-                after_first()
 
     def scatter_result(self, view, slot, half):
         total = view(self.pos, half)[...]
@@ -191,7 +189,7 @@
     def get(place):
         return decode(place[0][...], place[1][...])
 
-    def scatter(self, view, slot, staged, after_first=None):
+    def scatter(self, view, slot, staged):
         for direction, kind in self.each():
             place = staged(direction * 2 + kind)
             self.put(place, view(self.owner(direction, self.hops(kind)), self.half(direction, kind)))
@@ -208,8 +206,6 @@
                     self.put(slot(i), self.get(slot(i)) + own)
                     self.start_pair(slot(i), slot(i + 1), direction, kind, hop + 1)
             self.clock.spend(0.4)
-            if after_first is not None and (kind, hop) == (LONG, 1):
-                after_first()
 
     def scatter_result(self, view, slot, half):
         total = view(self.pos, half)
@@ -535,12 +531,12 @@
     def joined(ref, b, first, blocks):
         return ref[b, first : first + blocks].astype(f32).reshape(blocks * 8, RES).astype(bf16)
 
-    def colour_steps(layer, b, colour, after_first, done):
+    def colour_steps(layer, b, colour, done):
         place, group = places[colour], groups[b][colour]
         view, slot, staged = terms(place["view"](place["s"], b)), coded(*place["r"], b), coded(*place["e"], b)
         score(layer, b, colour)
         down = group["down"]
-        yield from down[0].scatter(view, slot, staged, after_first)
+        yield from down[0].scatter(view, slot, staged)
         last = place["last"].at[b]
         if colour == 0:
             for half in range(2):
@@ -589,15 +585,17 @@
             gains = gain_t[layer]
             normed = summed * lax.rsqrt(mean_sq + EPSILON) * jnp.concatenate([gains, gains], axis=1)
             x[s, :, block(b)] = normed.astype(bf16)
+            if layer + 1 == LAYERS:
+                far_out(b, s).start()
             return carry
 
         lax.fori_loop(0, 2, body, 0)
         clock.spend(1.5)
 
-    def far_out(b):
+    def far_out(b, s):
         return remote(
-            x.at[:, quarter(far_quarter), block(b)], out.at[pl.ds(near_pair, 2), :, block(b)],
-            o_send.at[b], o_recv.at[b], partner,
+            x.at[s, quarter(far_quarter), block(b)], out.at[near_pair + s, :, block(b)],
+            o_send.at[b, s], o_recv.at[b, s], partner,
         )
 
     def own_out(b):
@@ -606,7 +604,7 @@
         )
 
     def finish_steps(layer, b):
-        yield clock.now + 1.6
+        yield clock.now + (8.0 if b == 0 else 1.6)
         for colour in range(3):
             trade(layer, b, colour, 1 - core).wait_recv()
         finish(layer, b)
@@ -614,7 +612,6 @@
             project(layer + 1, 0, b)
             project(layer + 1, 1, b)
         else:
-            far_out(b).start()
             own_out(b).start()
 
     for layer in range(LAYERS):
@@ -629,20 +626,18 @@
         def launch(b, colour, layer=layer, add=add):
             left[b][colour] = 1
 
-            def after_first():
-                if b == 0:
-                    launch(1, colour)
-
             def done():
                 left[b][colour] = 0
                 if sum(left[b].values()) == 0 and len(left[b]) == 3:
                     add(finish_steps(layer, b))
 
-            add(colour_steps(layer, b, colour, after_first, done))
+            add(colour_steps(layer, b, colour, done))
 
         left = [{}, {}]
         for colour in range(3):
             launch(0, colour)
+        for colour in range(3):
+            launch(1, colour)
         for b in range(2):
             project(layer, 2, b)
         fillers = []
@@ -669,9 +664,10 @@
 
     for b in range(2):
         own_out(b).wait()
-        far_out(b).wait_send()
-        landed = out.at[pl.ds(far_pair, 2), :, block(b)]
-        remote(landed, landed, o_send.at[b], o_recv.at[b], partner).wait_recv()
+        for s in range(2):
+            far_out(b, s).wait_send()
+            landed = out.at[far_pair + s, :, block(b)]
+            remote(landed, landed, o_send.at[b, s], o_recv.at[b, s], partner).wait_recv()
 
 
 def on_device(tokens, qkv_weight, out_weight, norm_gain):
@@ -738,8 +734,8 @@
             dma((2, 3)),
             dma((LAYERS, 2, 3)),
             dma((2,)),
-            dma((2,)),
-            dma((2,)),
+            dma((2, 2)),
+            dma((2, 2)),
         ],
         compiler_params=pltpu.CompilerParams(
             collective_id=0, has_side_effects=True, vmem_limit_bytes=60 * 1024 * 1024

time: 155 us -> 146 us (0.942)
  Pallas kernels: 153 us -> 144 us
    pallas_call x1, Pallas kernels: 153 us -> 144 us  [on_device(): pl.pallas_call(functools.partial(whole, scale), out_shape=jax.ShapeDtypeS...]
where the time goes in v4:
time: 146 us
  Pallas kernels  144 us (99%)
  local copies, waits for them, and re-layouts  2.06 us (1%)
    pallas_call x1, Pallas kernels, on_device(): pl.pallas_call(functools.partial(whole, scale), out_shape=jax.ShapeDtypeS...  144 us

profile of v4, /device:TPU:1, one launch (start us, length us, event | category | flops | bytes accessed | tf_op | source)
XLA Modules:
  0.0 145.7 jit_solution(4013887013725397322)
XLA Ops:
  0.0 143.6 %shard_map.46 = bf16[4,192,512]{2,1,0:T(8,128)(2,1)} custom-call(bf16[4,192,512]{2,1,0:T(8,128)(2,1)} %bitcast.5, bf16[2,3,768,768]{3,2,1,0:T(8,128)(2,1)} %bitcast.3, bf16[2,768,768]{2,1,0:T(8,128)(2,1)} %wo.1, bf16[2,768]{1,0:T(2,128)(2,1)} %gain.1), custom_call_target="tpu_custom_call" | custom-call | tf_op jit(solution)/shard_map/pallas_call | solution.py:681
  143.6 2.1 %copy.6 = bf16[4,512,192]{1,2,0:T(8,128)(2,1)} copy(bf16[4,512,192]{1,2,0:T(8,128)(2,1)} %bitcast.4) | data formatting | bytes 1572864

commit v5 on v4

--- a/solution.py
+++ b/solution.py
@@ -604,7 +604,7 @@
         )
 
     def finish_steps(layer, b):
-        yield clock.now + (8.0 if b == 0 else 1.6)
+        yield clock.now + ((2.4, 2.4)[layer] if b == 0 else 1.6)
         for colour in range(3):
             trade(layer, b, colour, 1 - core).wait_recv()
         finish(layer, b)

time: 146 us -> 142 us (0.973)
  Pallas kernels: 144 us -> 140 us
    pallas_call x1, Pallas kernels: 144 us -> 140 us  [on_device(): pl.pallas_call(functools.partial(whole, scale), out_shape=jax.ShapeDtypeS...]
where the time goes in v5:
time: 142 us
  Pallas kernels  140 us (99%)
  local copies, waits for them, and re-layouts  2.06 us (1%)
    pallas_call x1, Pallas kernels, on_device(): pl.pallas_call(functools.partial(whole, scale), out_shape=jax.ShapeDtypeS...  140 us

profile of v5, /device:TPU:1, one launch (start us, length us, event | category | flops | bytes accessed | tf_op | source)
XLA Modules:
  0.0 142.4 jit_solution(16453182118104189878)
XLA Ops:
  0.0 140.4 %shard_map.46 = bf16[4,192,512]{2,1,0:T(8,128)(2,1)} custom-call(bf16[4,192,512]{2,1,0:T(8,128)(2,1)} %bitcast.5, bf16[2,3,768,768]{3,2,1,0:T(8,128)(2,1)} %bitcast.3, bf16[2,768,768]{2,1,0:T(8,128)(2,1)} %wo.1, bf16[2,768]{1,0:T(2,128)(2,1)} %gain.1), custom_call_target="tpu_custom_call" | custom-call | tf_op jit(solution)/shard_map/pallas_call | solution.py:681
  140.4 2.1 %copy.6 = bf16[4,512,192]{1,2,0:T(8,128)(2,1)} copy(bf16[4,512,192]{1,2,0:T(8,128)(2,1)} %bitcast.4) | data formatting | bytes 1572864

commit v6 on v5

--- a/solution.py
+++ b/solution.py
@@ -407,7 +407,6 @@
     for j in range(2, 4):
         arrived = piece(2 * (1 - xl) + 1 - core, *pieces[j])
         remote(arrived, arrived, f_send.at[j], f_recv.at[j], other_core).wait_recv()
-    project(0, 0, 1)
     project(0, 1, 1)
 
     def tokens_sent():
@@ -609,7 +608,8 @@
             trade(layer, b, colour, 1 - core).wait_recv()
         finish(layer, b)
         if layer + 1 < LAYERS:
-            project(layer + 1, 0, b)
+            if b == 0:
+                project(layer + 1, 0, b)
             project(layer + 1, 1, b)
         else:
             own_out(b).start()
@@ -636,6 +636,7 @@
         left = [{}, {}]
         for colour in range(3):
             launch(0, colour)
+        project(layer, 0, 1)
         for colour in range(3):
             launch(1, colour)
         for b in range(2):

time: 142 us -> 143 us (level); the launches traced: 142 us -> 142 us
  no operation moved by 1% of the time
where the time goes in v6:
time: 143 us; the launch traced here: 142 us
  Pallas kernels  140 us (98%)
  local copies, waits for them, and re-layouts  2.06 us (1%)
    pallas_call x1, Pallas kernels, on_device(): pl.pallas_call(functools.partial(whole, scale), out_shape=jax.ShapeDtypeS...  140 us

profile of v6, /device:TPU:1, one launch (start us, length us, event | category | flops | bytes accessed | tf_op | source)
XLA Modules:
  0.0 141.8 jit_solution(16641841930813574231)
XLA Ops:
  0.0 139.8 %shard_map.46 = bf16[4,192,512]{2,1,0:T(8,128)(2,1)} custom-call(bf16[4,192,512]{2,1,0:T(8,128)(2,1)} %bitcast.5, bf16[2,3,768,768]{3,2,1,0:T(8,128)(2,1)} %bitcast.3, bf16[2,768,768]{2,1,0:T(8,128)(2,1)} %wo.1, bf16[2,768]{1,0:T(2,128)(2,1)} %gain.1), custom_call_target="tpu_custom_call" | custom-call | tf_op jit(solution)/shard_map/pallas_call | solution.py:682
  139.8 2.1 %copy.6 = bf16[4,512,192]{1,2,0:T(8,128)(2,1)} copy(bf16[4,512,192]{1,2,0:T(8,128)(2,1)} %bitcast.4) | data formatting | bytes 1572864
